TPU v7x, 128 devices: a whole 4x4x4 slice. The times are simulated.
128 devices in a mesh: tiles: 16 (over y, z), rows: 8 (over x, core).
Axes of the slice: x: 4, y: 4, z: 4, core: 2. Of those that a mesh axis runs over, the one named last changes fastest.
Arguments:
- tile_values: bfloat16 [512, 128, 128, 128], P(('tiles', 'rows')), may hold values from -6 to 6
- tile_coords: int32 [256, 3], replicated, may hold values from 0 to 127, as said below
- tile_owner: int32 [256], replicated, may hold values from 0 to 127, as said below
- factor_b: bfloat16 [16384, 128], P('rows')
- factor_c: bfloat16 [16384, 128], P('rows')
Outputs:
- factor_a: float32 [16384, 128], P('rows')
Inputs may be any that keep to these rules, and one draw needn't show every extreme that they name: `tile_owner`: devices are numbered along tiles then rows. A device holds at most 4 tiles, and in every draw some device holds exactly 4; its tiles fill its first slots in increasing order of tile number. `tile_coords`: no two tiles have the same block indices.
All inputs are finite; a program needn't handle non-finite values.
Results may differ from a plain program's by a relative error of at most 0.0003.
Values may be sent and summed in bfloat16 or wider, within the bound.
No kernel may reach another device: no remote copies, remote signals or barrier semaphores. Data moves between devices by JAX's collectives and lax.ppermute only.
A program may use at most 128 MiB of HBM per device.

v0:
```python
import jax
import jax.numpy as jnp
from jax import lax
from jax.sharding import PartitionSpec as P


def slot_table(device, tile_coords, tile_owner, slot_count):
    mine = (tile_owner == device).astype(jnp.int32)
    order = jnp.cumsum(mine) - 1
    matches = (mine[None, :] == 1) & (
        order[None, :] == jnp.arange(slot_count, dtype=jnp.int32)[:, None]
    )
    present = jnp.any(matches, axis=1)
    placed = jnp.sum(matches.astype(jnp.int32)[:, :, None] * tile_coords[None, :, :], axis=1)
    return (placed, present)


def factor_gram(block_rows):
    return lax.dot_general(
        block_rows, block_rows, (((0,), (0,)), ((), ())), preferred_element_type=jnp.float32
    )


def body(tile_values, tile_coords, tile_owner, factor_b, factor_c):
    slot_count = tile_values.shape[0]
    tile_edge = tile_values.shape[1]
    rank_width = factor_b.shape[1]
    tiles_count = lax.axis_size("tiles")
    rows_count = lax.axis_size("rows")
    tiles_index = lax.axis_index("tiles")
    rows_index = lax.axis_index("rows")
    shard_rows = factor_b.shape[0]
    owned_rows = shard_rows // tiles_count
    blocks_unit = owned_rows // tile_edge
    edge_range = jnp.arange(tile_edge, dtype=jnp.int32)
    device = tiles_index * rows_count + rows_index
    coords, present = slot_table(device, tile_coords, tile_owner, slot_count)
    need_b = (coords[:, 1][:, None] * tile_edge + edge_range[None, :]).reshape(-1)
    need_c = (coords[:, 2][:, None] * tile_edge + edge_range[None, :]).reshape(-1)
    blank = jnp.zeros((slot_count * tile_edge, rank_width), jnp.bfloat16)
    carry = (blank, blank)
    pieces = (
        lax.all_gather(factor_b, "rows", axis=0, tiled=True),
        lax.all_gather(factor_c, "rows", axis=0, tiled=True),
    )
    results = []
    for held, piece, needed in zip(carry, pieces, (need_b, need_c)):
        inside = (needed >= 0) & (needed < piece.shape[0])
        taken = jnp.take(piece, jnp.clip(needed, 0, piece.shape[0] - 1), axis=0)
        results.append(jnp.where(inside[:, None], taken, held))
    chosen_b = results[0]
    chosen_c = results[1]

    def contract(position, partials):
        tile = lax.dynamic_index_in_dim(tile_values, position, 0, keepdims=False).reshape(
            tile_edge * tile_edge, tile_edge
        )
        block_c = lax.dynamic_slice_in_dim(chosen_c, position * tile_edge, tile_edge, 0)
        block_b = lax.dynamic_slice_in_dim(chosen_b, position * tile_edge, tile_edge, 0)
        inner = jnp.dot(tile, block_c, preferred_element_type=jnp.float32).reshape(
            tile_edge, tile_edge, rank_width
        )
        contrib = jnp.sum(inner * block_b.astype(jnp.float32)[None, :, :], axis=1)
        return lax.dynamic_update_index_in_dim(partials, contrib, position, 0)

    live_count = jnp.sum(present.astype(jnp.int32))
    partials = lax.fori_loop(
        0, live_count, contract, jnp.zeros((slot_count, tile_edge, rank_width), jnp.float32)
    )
    first_blocks = coords[:, 0]
    block_rows = jnp.arange(
        lax.axis_size(("tiles", "rows")) * owned_rows // tile_edge, dtype=jnp.int32
    )
    unit_index = block_rows // blocks_unit
    offset = block_rows % blocks_unit
    global_block = (
        unit_index % rows_count * tiles_count + unit_index // rows_count
    ) * blocks_unit + offset
    one_hot = ((global_block[:, None] == first_blocks[None, :]) & present[None, :]).astype(
        jnp.float32
    )
    summed = jnp.einsum("qs,sur->qur", one_hot, partials, precision=lax.Precision.HIGHEST)
    owned_sums = lax.psum_scatter(
        summed.reshape(lax.axis_size(("tiles", "rows")) * owned_rows, rank_width),
        ("tiles", "rows"),
        scatter_dimension=0,
        tiled=True,
    )
    gram_b, gram_c = lax.psum((factor_gram(factor_b), factor_gram(factor_c)), "rows")
    normal = gram_b * gram_c
    lower = jnp.linalg.cholesky(normal)
    solved = jax.scipy.linalg.cho_solve((lower, True), owned_sums.T).T
    return lax.all_gather(solved, "tiles", axis=0, tiled=True)


def solution(mesh):
    in_specs = (P(("tiles", "rows"), None, None, None), P(), P(), P("rows", None), P("rows", None))
    out_specs = P("rows", None)
    return jax.shard_map(body, mesh=mesh, in_specs=in_specs, out_specs=out_specs, check_vma=False)
```

profile of v0, /device:TPU:0, one launch (start us, length us, event | category | flops | bytes accessed | tf_op | source)
XLA Modules:
  0.0 838.5 jit_solution(6141258442397975768)
XLA Ops:
  6.5 0.0 all-gather.6.cloned.1.call-start
  6.5 0.7 all-gather.6.cloned.1.call-update
  7.3 0.0 all-gather.4.cloned.1.call-start
  7.3 0.7 all-gather.4.cloned.1.call-update
  8.0 0.0 all-reduce.3.cloned.1.call-start
  8.1 2.2 fusion.36
  10.2 2.2 fusion.37
  12.4 0.0 all-reduce.3.cloned.1.call-update
  12.4 0.0 reduce-scatter.2.cloned.1.call-start
  12.5 0.7 fusion.33
  13.2 0.3 reduce-window.9
  13.5 0.1 slice.34
  13.6 0.1 slice_reduce_fusion
  13.7 0.1 add_bitcast_fusion
  13.8 0.1 fusion.16
  13.9 0.8 multiply_reduce_fusion.1
  14.7 0.1 fusion.22
  14.8 0.1 compare_and_fusion
  14.9 0.1 compare_select_fusion
  15.0 0.1 compare_select_fusion.1
  15.1 0.6 convert_reduce_fusion
  15.7 27.9 %all-gather.6.cloned.1.call-done = bf16[16384,128]{1,0:T(8,128)(2,1)} async-done(((bf16[2048,128]{1,0:T(8,128)(2,1)}), bf16[16384,128]{1,0:T(8,128)(2,1)}) %all-gather.6.cloned.1.call-update) | async-done | bytes 4194320 | tf_op jit(solution)/shard_map/all_gather | solution.py:43
  43.6 3.8 gather_fusion.1
  47.4 0.2 select_select_fusion
  47.6 29.8 %all-gather.4.cloned.1.call-done = bf16[16384,128]{1,0:T(8,128)(2,1)} async-done(((bf16[2048,128]{1,0:T(8,128)(2,1)}), bf16[16384,128]{1,0:T(8,128)(2,1)}) %all-gather.4.cloned.1.call-update) | async-done | bytes 4194320 | tf_op jit(solution)/shard_map/all_gather | solution.py:44
  77.4 3.8 gather_fusion
  81.2 0.2 select_select_fusion.1
  81.5 0.8 while.10
  82.2 3.6 fusion.25
  85.8 8.1 copy.21
  93.9 0.0 reduce-scatter.2.cloned.1.call-update
  93.9 0.3 all-gather.8.cloned.1.call-start
  94.2 44.9 %all-reduce.3.cloned.1.call-done = (f32[128,128]{0,1:T(8,128)}, f32[128,128]{0,1:T(8,128)}) async-done(((f32[128,128]{0,1:T(8,128)}, f32[128,128]{0,1:T(8,128)}), (f32[128,128]{0,1:T(8,128)}, f32[128,128]{0,1:T(8,128)})) %all-reduce.3.cloned.1.call-update) | async-done | bytes 131088 | tf_op jit(solution)/shard_map/psum | solution.py:89
  139.1 0.9 mul.47
  140.0 0.1 copy.19
  140.1 11.7 %cholesky.16 = f32[128,128]{1,0:T(8,128)S(1)} custom-call(f32[128,128]{1,0:T(8,128)S(1)} %fusion.13), custom_call_target="Cholesky" | custom-call | tf_op jit(solution)/shard_map/jit(cholesky)/cholesky | solution.py:91
  151.8 0.6 compare_reduce_fusion
  152.5 0.7 fusion.8
  153.1 9.8 %custom-call.10 = f32[1,128,128]{1,2,0:T(8,128)S(1)} custom-call(f32[1,128,128]{2,1,0:T(8,128)S(1)} %fusion.8), custom_call_target="InvertDiagBlocksLowerTriangular" | custom-call | tf_op jit(solution)/shard_map/jit(_cho_solve)/triangular_solve | solution.py:92
  163.0 628.2 %reduce-scatter.2.cloned.1.call-done = f32[128,128]{1,0:T(8,128)} async-done(((f32[16384,128]{1,0:T(8,128)}), f32[128,128]{1,0:T(8,128)}) %reduce-scatter.2.cloned.1.call-update) | async-done | bytes 65552 | tf_op jit(solution)/shard_map/reduce_scatter | solution.py:83
  791.2 1.1 fusion.11
  792.3 0.9 fusion.9
  793.2 0.0 all-gather.8.cloned.1.call-update
  793.3 36.5 %all-gather.8.cloned.1.call-done = f32[2048,128]{1,0:T(8,128)} async-done(((f32[128,128]{1,0:T(8,128)}), f32[2048,128]{1,0:T(8,128)}) %all-gather.8.cloned.1.call-update) | async-done | bytes 1048592 | tf_op jit(solution)/shard_map/all_gather | solution.py:93
  829.7 2.3 copy.37
  (8 shorter events, 0.1 us)
Async XLA Ops:
  6.5 37.1 %all-gather.6.cloned.1.call-start = ((), (), s32[]{:S(2)}) async-start(), calls=%async_computation.2 | async-start | bytes 4718592 | tf_op jit(solution)/shard_map/all_gather | solution.py:43
  7.3 70.2 %all-gather.4.cloned.1.call-start = ((), (), s32[]{:S(2)}) async-start(), calls=%async_computation.1 | async-start | bytes 4718592 | tf_op jit(solution)/shard_map/all_gather | solution.py:44
  8.0 131.1 %all-reduce.3.cloned.1.call-start = ((), (), s32[]{:S(2)}) async-start(), calls=%async_computation.5 | async-start | bytes 262144 | tf_op jit(solution)/shard_map/psum | solution.py:89
  12.4 778.8 %reduce-scatter.2.cloned.1.call-start = ((), (), s32[]{:S(2)}) async-start(), calls=%async_computation.3 | async-start | bytes 8454144 | tf_op jit(solution)/shard_map/reduce_scatter | solution.py:83
  93.9 735.8 %all-gather.8.cloned.1.call-start = ((), (), s32[]{:S(2)}) async-start(), calls=%async_computation.4 | async-start | bytes 1114112 | tf_op jit(solution)/shard_map/all_gather | solution.py:93
Sparse Core Ops, SparseCore 0:
  9.1 34.5 all-gather.5
  45.4 32.0 all-gather.3
  79.8 59.2 all-reduce.2
  141.4 649.7 reduce-scatter.1
  793.4 36.3 all-gather.7
where the time goes:
time: 839 us
  waiting for transfers between devices  769 us (92%)
  other arithmetic  27.2 us (3%)
  local copies, waits for them, and re-layouts  18.2 us (2%)
  between operations  13.3 us (2%)
  matrix products  9.95 us (1%)
    reduce_scatter x1, waiting for transfers between devices, body(): lax.psum_scatter(summed.reshape(lax.axis_size(('tiles', 'rows')) * owned_...  628 us
    psum x1, waiting for transfers between devices, body(): lax.psum((factor_gram(factor_b), factor_gram(factor_c)), 'rows')  44.9 us
    all_gather x1, waiting for transfers between devices, body(): return lax.all_gather(solved, 'tiles', axis=0, tiled=True)  36.5 us
    all_gather x1, waiting for transfers between devices, body(): lax.all_gather(factor_c, 'rows', axis=0, tiled=True)  29.8 us
    all_gather x1, waiting for transfers between devices, body(): lax.all_gather(factor_b, 'rows', axis=0, tiled=True)  27.9 us
  transfers between devices with their start and end apart: 5, of which 5 were waited for; matrix products, arithmetic and copies ran while one was open for 6% of the time, Pallas kernels for 0%

commit v1 on v0

v1 whole, which is shorter than its diff:
```python
import jax
import jax.numpy as jnp
from jax import lax
from jax.experimental import pallas as pl
from jax.experimental.pallas import tpu as pltpu
from jax.sharding import PartitionSpec as P

F32 = jnp.float32
BF16 = jnp.bfloat16
HIGHEST = lax.Precision.HIGHEST
STRIP = 8
PRESENT = 21
CHUNK = 16
BUFFERS = 8


def split3(x):
    hi = x.astype(BF16)
    rest = x - hi.astype(F32)
    mid = rest.astype(BF16)
    lo = (rest - mid.astype(F32)).astype(BF16)
    return hi, mid, lo


def join3(hi, mid, lo):
    return (lo.astype(F32) + mid.astype(F32)) + hi.astype(F32)


def vmem():
    return pl.BlockSpec(memory_space=pltpu.VMEM)


def smem():
    return pl.BlockSpec(memory_space=pltpu.SMEM)


def hbm():
    return pl.BlockSpec(memory_space=pl.ANY)


def slot_codes(tile_coords, tile_owner, slot_count, rows_count, tiles_count, rows_index):
    tiles = tile_owner.shape[0]
    number = jnp.arange(tiles, dtype=jnp.int32)
    earlier = (tile_owner[None, :] == tile_owner[:, None]) & (number[None, :] < number[:, None])
    order = jnp.sum(earlier.astype(jnp.int32), axis=1)
    slot = tile_owner * slot_count + order
    code = (
        tile_coords[:, 0]
        + (tile_coords[:, 1] << 7)
        + (tile_coords[:, 2] << 14)
        + (1 << PRESENT)
    )
    place = jnp.arange(tiles_count * slot_count, dtype=jnp.int32)
    wanted = ((place // slot_count) * rows_count + rows_index) * slot_count + place % slot_count
    return jnp.sum(jnp.where(slot[None, :] == wanted[:, None], code[None, :], 0), axis=1)


def pack_factors(fb_ref, fc_ref, sb_ref, sc_ref, out_ref, strips, gram, sem):
    t = lax.axis_index("tiles")
    blocks = sb_ref.shape[0]
    copies = [
        pltpu.make_async_copy(sb_ref.at[:, t], strips.at[pl.ds(0, blocks)], sem.at[0]),
        pltpu.make_async_copy(sc_ref.at[:, t], strips.at[pl.ds(blocks, blocks)], sem.at[1]),
    ]
    for copy in copies:
        copy.start()
    parts = []
    for at, ref in enumerate((fb_ref, fc_ref)):
        rows = ref[...]
        gram[at] = lax.dot_general(rows, rows, (((0,), (0,)), ((), ())), preferred_element_type=F32)
        parts.extend(split3(gram[at, pl.ds(pl.multiple_of(t * STRIP, STRIP), STRIP), :]))
    for copy in copies:
        copy.wait()
    held = strips[...]
    for d in range(out_ref.shape[0]):
        out_ref[d, 0 : 2 * blocks] = held
        for at, part in enumerate(parts):
            out_ref[d, 2 * blocks + at] = part


def route_factors(code_ref, in_ref, out_ref, *, slots):
    sources = in_ref.shape[0]
    blocks = (in_ref.shape[1] - 6) // 2
    for d in range(out_ref.shape[0]):
        for s in range(slots):
            code = code_ref[d * slots + s]
            j = (code >> 7) & 127
            k = (code >> 14) & 127
            out_ref[d, s] = in_ref[j // blocks, j % blocks]
            out_ref[d, slots + s] = in_ref[k // blocks, blocks + k % blocks]
    grams = []
    for at in range(2):
        base = 2 * blocks + 3 * at
        total = None
        for q in range(sources):
            piece = join3(in_ref[q, base], in_ref[q, base + 1], in_ref[q, base + 2])
            total = piece if total is None else total + piece
        grams.append(total)
    for at, part in enumerate(split3(grams[0] * grams[1])):
        for d in range(out_ref.shape[0]):
            out_ref[d, 2 * slots + at] = part


def contract(code_ref, x_ref, in_ref, out_ref, normal_ref, buf, bs, cs, sem, *, slots):
    t = lax.axis_index("tiles")
    edge = x_ref.shape[1]
    per_tile = edge // CHUNK
    strips = edge // STRIP
    live = code_ref[t * slots] >> PRESENT
    for s in range(1, slots):
        live = live + (code_ref[t * slots + s] >> PRESENT)
    chunks = live * per_tile

    def fetch(c):
        s = c // per_tile
        a = (c % per_tile) * CHUNK
        slot = c % BUFFERS
        return pltpu.make_async_copy(
            x_ref.at[s, pl.ds(a, CHUNK)], buf.at[slot], sem.at[slot]
        )

    for c in range(BUFFERS):
        @pl.when(c < chunks)
        def _():
            fetch(jnp.int32(c)).start()

    for s in range(slots):
        for u in range(strips):
            bs[s, pl.ds(u * STRIP, STRIP), :] = in_ref[u, s].astype(F32)
            cs[s, pl.ds(u * STRIP, STRIP), :] = in_ref[u, slots + s].astype(F32)
    for u in range(strips):
        normal_ref[pl.ds(u * STRIP, STRIP), :] = join3(
            in_ref[u, 2 * slots], in_ref[u, 2 * slots + 1], in_ref[u, 2 * slots + 2]
        )
    out_ref[...] = jnp.zeros_like(out_ref)

    def step(c, carry):
        s = c // per_tile
        slot = c % BUFFERS
        fetch(c).wait()
        x = buf[slot].reshape(CHUNK * edge, edge)
        inner = jnp.dot(x, cs[s].astype(BF16), preferred_element_type=F32)
        inner = inner.reshape(CHUNK, edge, edge) * bs[s][None]
        total = jnp.sum(inner, axis=1)
        for u in range(CHUNK // STRIP):
            out_ref[(c % per_tile) * (CHUNK // STRIP) + u, s] = total[u * STRIP : (u + 1) * STRIP]

        @pl.when(c + BUFFERS < chunks)
        def _():
            fetch(c + BUFFERS).start()

        return carry

    lax.fori_loop(0, chunks, step, 0)


def gather_blocks(code_ref, in_ref, out_ref, *, slots):
    out_ref[...] = jnp.zeros_like(out_ref)
    blocks = out_ref.shape[1]
    for d in range(in_ref.shape[0]):
        for s in range(slots):
            code = code_ref[d * slots + s]
            i = code & 127
            here = (code >> PRESENT) > 0
            value = jnp.where(here, in_ref[d, s], 0.0)
            out_ref[i // blocks, i % blocks] += value


def solve(in_ref, inv_ref, out_ref):
    total = in_ref[0]
    for q in range(1, in_ref.shape[0]):
        total = total + in_ref[q]
    rows = total.reshape(total.shape[0] * STRIP, total.shape[2])
    inv = inv_ref[...]
    first = lax.dot_general(
        rows, inv, (((1,), (1,)), ((), ())), precision=HIGHEST, preferred_element_type=F32
    )
    second = jnp.dot(first, inv, precision=HIGHEST, preferred_element_type=F32)
    second = second.reshape(total.shape)
    for d in range(out_ref.shape[0]):
        out_ref[d] = second


def body(tile_values, tile_coords, tile_owner, factor_b, factor_c):
    slots = tile_values.shape[0]
    edge = tile_values.shape[1]
    rank = factor_b.shape[1]
    shard = factor_b.shape[0]
    tiles_count = lax.axis_size("tiles")
    rows_count = lax.axis_size("rows")
    rows_index = lax.axis_index("rows")
    blocks = shard // edge
    strips = edge // STRIP
    tile = (STRIP, rank)

    packed = pl.pallas_call(
        pack_factors,
        name="pack_factors",
        out_shape=jax.ShapeDtypeStruct((rows_count, 2 * blocks + 6) + tile, BF16),
        in_specs=[vmem(), vmem(), hbm(), hbm()],
        out_specs=vmem(),
        scratch_shapes=[
            pltpu.VMEM((2 * blocks,) + tile, BF16),
            pltpu.VMEM((2, rank, rank), F32),
            pltpu.SemaphoreType.DMA((2,)),
        ],
    )(
        factor_b,
        factor_c,
        factor_b.reshape((blocks, strips) + tile),
        factor_c.reshape((blocks, strips) + tile),
    )
    codes = slot_codes(tile_coords, tile_owner, slots, rows_count, tiles_count, rows_index)
    spread = lax.all_to_all(packed, "rows", 0, 0, tiled=True)
    routed = pl.pallas_call(
        lambda *refs: route_factors(*refs, slots=slots),
        name="route_factors",
        out_shape=jax.ShapeDtypeStruct((tiles_count, 2 * slots + 3) + tile, BF16),
        in_specs=[smem(), vmem()],
        out_specs=vmem(),
    )(codes, spread)
    chosen = lax.all_to_all(routed, "tiles", 0, 0, tiled=True)
    partials, normal = pl.pallas_call(
        lambda *refs: contract(*refs, slots=slots),
        name="contract",
        out_shape=(
            jax.ShapeDtypeStruct((tiles_count, slots) + tile, F32),
            jax.ShapeDtypeStruct((rank, rank), F32),
        ),
        in_specs=[smem(), hbm(), vmem()],
        out_specs=(vmem(), vmem()),
        scratch_shapes=[
            pltpu.VMEM((BUFFERS, CHUNK, edge, edge), BF16),
            pltpu.VMEM((slots, edge, rank), F32),
            pltpu.VMEM((slots, edge, rank), F32),
            pltpu.SemaphoreType.DMA((BUFFERS,)),
        ],
        compiler_params=pltpu.CompilerParams(vmem_limit_bytes=32 << 20),
    )(codes, tile_values, chosen)
    moved = lax.all_to_all(partials, "tiles", 0, 0, tiled=True)
    lower = jnp.linalg.cholesky(normal)
    inverse = lax.linalg.triangular_solve(
        lower, jnp.eye(rank, dtype=F32), left_side=True, lower=True
    )
    dense = pl.pallas_call(
        lambda *refs: gather_blocks(*refs, slots=slots),
        name="gather_blocks",
        out_shape=jax.ShapeDtypeStruct((rows_count, blocks) + tile, F32),
        in_specs=[smem(), vmem()],
        out_specs=vmem(),
    )(codes, moved)
    owned = lax.all_to_all(dense, "rows", 0, 0, tiled=True)
    solved = pl.pallas_call(
        solve,
        name="solve",
        out_shape=jax.ShapeDtypeStruct((tiles_count, blocks) + tile, F32),
        in_specs=[vmem(), vmem()],
        out_specs=vmem(),
    )(owned, inverse)
    full = lax.all_to_all(solved, "tiles", 0, 0, tiled=True)
    return full.transpose(1, 0, 2, 3).reshape(shard, rank)


def solution(mesh):
    in_specs = (P(("tiles", "rows"), None, None, None), P(), P(), P("rows", None), P("rows", None))
    out_specs = P("rows", None)
    return jax.shard_map(body, mesh=mesh, in_specs=in_specs, out_specs=out_specs, check_vma=False)
```

time: 839 us -> 122 us (0.15)
  waiting for transfers between devices: 769 us -> 8.24 us
  blocking collectives: 0 us -> 42.2 us
  Pallas kernels: 0 us -> 22.5 us
  between operations: 13.3 us -> 0.09 us
  starting transfers between devices: 0.38 us -> 11.4 us
  matrix products: 9.95 us -> 0.89 us
    reduce_scatter x1 -> x0, waiting for transfers between devices: 628 us -> none  [body(): lax.psum_scatter(summed.reshape(lax.axis_size(('tiles', 'rows')) * owned_...]
    all_gather x3 -> x0, waiting for transfers between devices: 94.2 us -> none  [the longest x1 36.5 us: body(): return lax.all_gather(solved, 'tiles', axis=0, tiled=True)]
    psum x1 -> x0, waiting for transfers between devices: 44.9 us -> none  [body(): lax.psum((factor_gram(factor_b), factor_gram(factor_c)), 'rows')]
    all_to_all x0 -> x2, blocking collectives: none -> 42.2 us  [the longest x1 24.9 us: body(): full = lax.all_to_all(solved, 'tiles', 0, 0, tiled=True)]
    pallas_call x0 -> x5, Pallas kernels: none -> 22.5 us  [the longest x1 12.4 us: body(): pl.pallas_call(lambda *refs: contract(*refs, slots=slots), name='contract...]
    all_to_all x0 -> x3, starting transfers between devices: none -> 11.4 us  [the longest x1 4.4 us: body(): spread = lax.all_to_all(packed, 'rows', 0, 0, tiled=True)]
  transfers between devices with their start and end apart: 5 -> 3, of which waited for: 5 -> 1; matrix products, arithmetic and copies ran while one was open for 6% -> 22% of each run, Pallas kernels for 0% -> 0%
where the time goes in v1:
time: 122 us; the launch traced here: 121 us
  blocking collectives  42.2 us (35%)
  other arithmetic  25.9 us (21%)
  Pallas kernels  22.5 us (18%)
  starting transfers between devices  11.4 us (9%)
  local copies, waits for them, and re-layouts  9.87 us (8%)
  waiting for transfers between devices  8.24 us (7%)
    all_to_all x1, blocking collectives, body(): full = lax.all_to_all(solved, 'tiles', 0, 0, tiled=True)  24.9 us
    all_to_all x1, blocking collectives, body(): chosen = lax.all_to_all(routed, 'tiles', 0, 0, tiled=True)  17.3 us
    pallas_call x1, Pallas kernels, body(): pl.pallas_call(lambda *refs: contract(*refs, slots=slots), name='contract...  12.4 us
    another operation x3, other arithmetic, body(): lower = jnp.linalg.cholesky(normal)  12.4 us
    another operation x2, other arithmetic, body(): lax.linalg.triangular_solve(lower, jnp.eye(rank, dtype=F32), left_side=Tr...  10.4 us
    unnamed x10, local copies, waits for them, and re-layouts  8.7 us
    all_to_all x1, waiting for transfers between devices, body(): spread = lax.all_to_all(packed, 'rows', 0, 0, tiled=True)  8.24 us
    all_to_all x1, starting transfers between devices, body(): spread = lax.all_to_all(packed, 'rows', 0, 0, tiled=True)  4.4 us
  transfers between devices with their start and end apart: 3, of which 1 were waited for; matrix products, arithmetic and copies ran while one was open for 22% of the time, Pallas kernels for 0%

profile of v1, /device:TPU:0, one launch (start us, length us, event | category | flops | bytes accessed | tf_op | source)
XLA Modules:
  0.0 121.1 jit_solution(14487112028314857100)
XLA Ops:
  0.0 2.9 %pack_factors.1 = bf16[8,38,8,128]{3,2,1,0:T(8,128)(2,1)} custom-call(bf16[2048,128]{1,0:T(8,128)(2,1)} %fb_ref.1, bf16[2048,128]{1,0:T(8,128)(2,1)} %fc_ref.1, bf16[16,16,8,128]{3,2,1,0:T(8,128)(2,1)} %bitcast.15, bf16[16,16,8,128]{3,2,1,0:T(8,128)(2,1)} %bitcast.16), custom_call_target="tpu_custom_call" | custom-call | tf_op jit(solution)/shard_map/pack_factors/pallas_call | solution.py:196
  2.9 4.4 %all-to-all-start = ((bf16[8,38,8,128]{3,2,1,0:T(8,128)(2,1)}), bf16[8,38,8,128]{3,2,1,0:T(8,128)(2,1)S(1)}, u32[]{:S(2)}, u32[]{:S(2)}) async-start(bf16[8,38,8,128]{3,2,1,0:T(8,128)(2,1)} %pack_factors.1), calls=%async_computation | async-start | bytes 1245184 | tf_op jit(solution)/shard_map/all_to_all | solution.py:214
  7.3 0.9 convert_reduce_fusion
  8.2 0.7 multiply_add_fusion
  8.9 0.8 add_add_fusion
  9.7 0.7 select_reduce_fusion.1.refs_0_
  10.5 8.2 %all-to-all-done.refs_1_ = bf16[8,38,8,128]{3,2,1,0:T(8,128)(2,1)S(1)} async-done(((bf16[8,38,8,128]{3,2,1,0:T(8,128)(2,1)}), bf16[8,38,8,128]{3,2,1,0:T(8,128)(2,1)S(1)}, u32[]{:S(2)}, u32[]{:S(2)}) %all-to-all-start) | async-done | bytes 622624 | tf_op jit(solution)/shard_map/all_to_all | solution.py:214
  18.7 0.0 copy-start.2
  18.7 0.8 copy-done.2
  19.5 2.4 %route_factors.1 = bf16[16,11,8,128]{3,2,1,0:T(8,128)(2,1)} custom-call(s32[64]{0:T(128)} %select_reduce_fusion.1.refs_0_, bf16[8,38,8,128]{3,2,1,0:T(8,128)(2,1)} %copy-done.2), custom_call_target="tpu_custom_call" | custom-call | tf_op jit(solution)/shard_map/route_factors/pallas_call | solution.py:215
  22.0 17.3 %all_to_all.25.refs_2_ = bf16[16,11,8,128]{3,2,1,0:T(8,128)(2,1)S(1)} all-to-all(bf16[16,11,8,128]{3,2,1,0:T(8,128)(2,1)} %route_factors.1), channel_id=1, replica_groups=mesh['tiles'=16,'rows'=8] {'tiles'}, dimensions={0} | all-to-all | bytes 720896 | tf_op jit(solution)/shard_map/all_to_all | solution.py:222
  39.3 0.0 copy-start
  39.3 5.8 %copy-done = bf16[4,128,128,128]{3,2,1,0:T(8,128)(2,1)S(1)} copy-done((bf16[4,128,128,128]{3,2,1,0:T(8,128)(2,1)S(1)}, bf16[4,128,128,128]{3,2,1,0:T(8,128)(2,1)}, u32[]{:S(2)}) %copy-start) | copy-done | bytes 16777240
  45.1 0.0 copy-start.1
  45.1 0.6 copy-done.1
  45.7 12.4 %contract.1 = (f32[16,4,8,128]{3,2,1,0:T(8,128)}, f32[128,128]{1,0:T(8,128)S(1)}) custom-call(s32[64]{0:T(128)S(1)} %copy-done.1, bf16[4,128,128,128]{3,2,1,0:T(8,128)(2,1)S(1)} %copy-done, bf16[16,11,8,128]{3,2,1,0:T(8,128)(2,1)S(1)} %all_to_all.25.refs_2_), custom_call_target="tpu_custom_call" | custom-call | tf_op jit(solution)/shard_map/contract/pallas_call | solution.py:223
  58.1 3.5 %all-to-all-start.2 = ((f32[16,4,8,128]{3,2,1,0:T(8,128)}), f32[16,4,8,128]{3,2,1,0:T(8,128)S(1)}, u32[]{:S(2)}, u32[]{:S(2)}) async-start(f32[16,4,8,128]{3,2,1,0:T(8,128)} %get-tuple-element.7), calls=%async_computation.2 | async-start | bytes 524288 | tf_op jit(solution)/shard_map/all_to_all | solution.py:240
  61.7 0.1 copy.9
  61.8 11.7 %cholesky.17 = f32[128,128]{1,0:T(8,128)S(1)} custom-call(f32[128,128]{1,0:T(8,128)S(1)} %fusion.4), custom_call_target="Cholesky" | custom-call | tf_op jit(solution)/shard_map/jit(cholesky)/cholesky | solution.py:241
  73.5 0.0 all-to-all-done.2.refs_1_
  73.6 0.0 copy-start.4
  73.6 0.7 copy-done.4
  74.3 2.1 %gather_blocks.1 = f32[8,16,8,128]{3,2,1,0:T(8,128)} custom-call(s32[64]{0:T(128)} %select_reduce_fusion.1.refs_0_, f32[16,4,8,128]{3,2,1,0:T(8,128)} %copy-done.4), custom_call_target="tpu_custom_call" | custom-call | tf_op jit(solution)/shard_map/gather_blocks/pallas_call | solution.py:245
  76.4 3.5 %all-to-all-start.3 = ((f32[8,16,8,128]{3,2,1,0:T(8,128)}), f32[8,16,8,128]{3,2,1,0:T(8,128)S(1)}, u32[]{:S(2)}, u32[]{:S(2)}) async-start(f32[8,16,8,128]{3,2,1,0:T(8,128)} %gather_blocks.1), calls=%async_computation.3 | async-start | bytes 1048576 | tf_op jit(solution)/shard_map/all_to_all | solution.py:252
  79.9 0.6 compare_reduce_fusion
  80.5 0.6 fusion.1
  81.1 9.8 %custom-call.6 = f32[1,128,128]{1,2,0:T(8,128)S(1)} custom-call(f32[1,128,128]{2,1,0:T(8,128)S(1)} %fusion.1), custom_call_target="InvertDiagBlocksLowerTriangular" | custom-call | tf_op jit(solution)/shard_map/triangular_solve | solution.py:242
  90.9 0.9 fusion.2.inv_ref
  91.8 0.0 all-to-all-done.3.in_ref
  91.8 0.0 copy-start.3
  91.8 0.8 copy-done.3
  92.6 2.6 %solve.1 = f32[16,16,8,128]{3,2,1,0:T(8,128)} custom-call(f32[8,16,8,128]{3,2,1,0:T(8,128)} %copy-done.3, f32[128,128]{1,0:T(8,128)} %fusion.2.inv_ref), custom_call_target="tpu_custom_call" | custom-call | tf_op jit(solution)/shard_map/solve/pallas_call | solution.py:253
  95.2 24.9 %all_to_all.26 = f32[16,16,8,128]{3,2,1,0:T(8,128)S(1)} all-to-all(f32[16,16,8,128]{3,2,1,0:T(8,128)} %solve.1), channel_id=1, replica_groups=mesh['tiles'=16,'rows'=8] {'tiles'}, dimensions={0} | all-to-all | bytes 2097152 | tf_op jit(solution)/shard_map/all_to_all | solution.py:260
  120.1 1.1 copy.10
  (3 shorter events, 0.1 us)
Async XLA Ops:
  2.9 15.8 %all-to-all-start = ((bf16[8,38,8,128]{3,2,1,0:T(8,128)(2,1)}), bf16[8,38,8,128]{3,2,1,0:T(8,128)(2,1)S(1)}, u32[]{:S(2)}, u32[]{:S(2)}) async-start(bf16[8,38,8,128]{3,2,1,0:T(8,128)(2,1)} %pack_factors.1), calls=%async_computation | async-start | bytes 1245184 | tf_op jit(solution)/shard_map/all_to_all | solution.py:214
  18.7 0.8 copy-start.2
  39.3 5.8 %copy-start = (bf16[4,128,128,128]{3,2,1,0:T(8,128)(2,1)S(1)}, bf16[4,128,128,128]{3,2,1,0:T(8,128)(2,1)}, u32[]{:S(2)}) copy-start(bf16[4,128,128,128]{3,2,1,0:T(8,128)(2,1)} %refs_1_.1) | copy-start | bytes 50331652
  45.1 0.6 copy-start.1
  58.1 15.4 %all-to-all-start.2 = ((f32[16,4,8,128]{3,2,1,0:T(8,128)}), f32[16,4,8,128]{3,2,1,0:T(8,128)S(1)}, u32[]{:S(2)}, u32[]{:S(2)}) async-start(f32[16,4,8,128]{3,2,1,0:T(8,128)} %get-tuple-element.7), calls=%async_computation.2 | async-start | bytes 524288 | tf_op jit(solution)/shard_map/all_to_all | solution.py:240
  73.6 0.7 copy-start.4
  76.4 15.4 %all-to-all-start.3 = ((f32[8,16,8,128]{3,2,1,0:T(8,128)}), f32[8,16,8,128]{3,2,1,0:T(8,128)S(1)}, u32[]{:S(2)}, u32[]{:S(2)}) async-start(f32[8,16,8,128]{3,2,1,0:T(8,128)} %gather_blocks.1), calls=%async_computation.3 | async-start | bytes 1048576 | tf_op jit(solution)/shard_map/all_to_all | solution.py:252
  91.8 0.8 copy-start.3

commit v2 on v0

v2 whole, which is shorter than its diff:
```python
import jax
import jax.numpy as jnp
from jax import lax
from jax.experimental import pallas as pl
from jax.experimental.pallas import tpu as pltpu
from jax.sharding import PartitionSpec as P

F32 = jnp.float32
BF16 = jnp.bfloat16
HIGHEST = lax.Precision.HIGHEST
STRIP = 8
PRESENT = 21
CHUNK = 16
PARTS = 4
LANES = 128
BITS = 15.0
FULL = 32768.0
TINY = 2.0**-111
CAPACITIES = (6, 2)
CORES = 2
SMALL = pl.CostEstimate(flops=1024, bytes_accessed=1024, transcendentals=0)
LIMIT = pltpu.CompilerParams(vmem_limit_bytes=8 << 20)


def vmem():
    return pl.BlockSpec(memory_space=pltpu.VMEM)


def smem():
    return pl.BlockSpec(memory_space=pltpu.SMEM)


def hbm():
    return pl.BlockSpec(memory_space=pl.ANY)


def in_hbm(x):
    return pltpu.with_memory_space_constraint(x, pltpu.HBM)


def coord_i(code):
    return code & 127


def coord_j(code):
    return (code >> 7) & 127


def coord_k(code):
    return (code >> 14) & 127


def present(code):
    return code >> PRESENT


def plan(owner_hbm, coords_hbm, code_ref, rounds_ref, owner_ref, coords_ref, sem, *, slots, rows_count, blocks):
    t = lax.axis_index("tiles")
    r = lax.axis_index("rows")
    tiles = owner_ref.shape[1]
    chips = rows_count // CORES
    shift = (blocks * CORES).bit_length() - 1
    loads = [
        pltpu.make_async_copy(owner_hbm, owner_ref, sem.at[0]),
        pltpu.make_async_copy(coords_hbm, coords_ref, sem.at[1]),
    ]
    for load in loads:
        load.start()
    for load in loads:
        load.wait()
    owner = owner_ref[...]
    coords = coords_ref[...]
    first, second, third = coords[0:1], coords[1:2], coords[2:3]
    code = first + (second << 7) + (third << 14) + (1 << PRESENT)
    key_b = owner * chips + (second >> shift)
    key_c = owner * chips + (third >> shift)
    lanes = jnp.concatenate([owner, code, key_b, key_c, owner, code, key_b, key_c], axis=0)
    columns = jnp.transpose(lanes)
    owner_at, code_at = columns[:, 0:1], columns[:, 1:2]
    key_b_at, key_c_at = columns[:, 2:3], columns[:, 3:4]
    square = (tiles, tiles)
    number_at = lax.broadcasted_iota(jnp.int32, square, 0)
    number = lax.broadcasted_iota(jnp.int32, square, 1)
    one = jnp.ones(square, jnp.int32)
    zero = jnp.zeros(square, jnp.int32)
    earlier = jnp.where((owner_at == owner) & (number < number_at), one, zero)
    slot_at = owner_at * slots + jnp.sum(earlier, axis=1, keepdims=True)
    place = lax.broadcasted_iota(jnp.int32, (1, LANES), 1)
    within = place % slots
    column = ((place // slots) * rows_count + r) * slots + within
    row = (t * rows_count + (place - 64) // slots) * slots + within
    wanted = jnp.where(place < 64, column, jnp.where(place < 96, row, -1))
    code_ref[...] = jnp.sum(jnp.where(slot_at == wanted, code_at, 0), axis=0, keepdims=True)
    most = jnp.zeros((1, 1), jnp.int32)
    for key_at in (key_b_at, key_c_at):
        same = jnp.where(key_at == key_b, one, zero) + jnp.where(key_at == key_c, one, zero)
        most = jnp.maximum(most, jnp.max(jnp.sum(same, axis=1, keepdims=True), axis=0, keepdims=True))
    rounds = jnp.zeros((1, 1), jnp.int32)
    base = 0
    for capacity in CAPACITIES[:-1]:
        base = base + capacity
        rounds = rounds + jnp.where(most > base, 1, 0)
    rounds_ref[0, 0] = jnp.sum(rounds)


def gather_factors(code_ref, fb_ref, fc_ref, sb_ref, sc_ref, *refs, slots):
    outs, sem = refs[:-1], refs[-1]
    r = lax.axis_index("rows")
    blocks = fb_ref.shape[0]
    count = jnp.int32(0)
    for x in range(outs[0].shape[0]):
        at = jnp.int32(0)
        for s in range(slots):
            code = code_ref[0, 64 + (x * CORES + r % CORES) * slots + s]
            for own, sibling, coord in ((fb_ref, sb_ref, coord_j(code)), (fc_ref, sc_ref, coord_k(code))):
                shard = coord // blocks
                hit = (present(code) > 0) & (shard // CORES == r // CORES)
                base = 0
                for out, capacity in zip(outs, CAPACITIES):
                    if base >= 2 * s + 2:
                        break
                    inside = hit & (at >= base) & (at < base + capacity)
                    for ref, held in ((own, shard == r), (sibling, shard != r)):

                        @pl.when(inside & held)
                        def _(ref=ref, coord=coord, at=at, x=x, out=out, base=base):
                            pltpu.make_async_copy(
                                ref.at[coord % blocks], out.at[x, at - base], sem
                            ).start()

                    base = base + capacity
                at = at + hit.astype(jnp.int32)
        count = count + at

    def drain(_, carry):
        pltpu.make_async_copy(fb_ref.at[0], outs[0].at[0, 0], sem).wait()
        return carry

    lax.fori_loop(0, count, drain, 0)


def chip_gram(fb_ref, fc_ref, sb_ref, sc_ref, out_ref, buf, sem):
    core = lax.axis_index("rows") % CORES
    over = (((0,), (0,)), ((), ()))
    for which, (own, sibling) in enumerate(((fb_ref, sb_ref), (fc_ref, sc_ref))):

        @pl.when(core == which)
        def _(own=own, sibling=sibling):
            copies = [
                pltpu.make_async_copy(ref, buf.at[at], sem.at[at])
                for at, ref in enumerate((own, sibling))
            ]
            for copy in copies:
                copy.start()
            for copy in copies:
                copy.wait()

    out_ref[...] = sum(
        lax.dot_general(buf[at], buf[at], over, preferred_element_type=F32) for at in range(CORES)
    )


def contract(code_ref, x_ref, *refs, slots, blocks):
    ins = refs[: len(CAPACITIES)]
    out_ref, buf, bs, cs, scalar_ref, code_sem, sem = refs[len(CAPACITIES) :]
    r = lax.axis_index("rows")
    edge = x_ref.shape[1]
    part = edge // PARTS

    def fetch(s, q):
        rows = pl.ds(q * part, part)
        return pltpu.make_async_copy(x_ref.at[s, rows], buf.at[s, rows], sem.at[s, q])

    codes_copy = pltpu.make_async_copy(code_ref, scalar_ref, code_sem)
    codes_copy.start()
    for s in range(slots):
        for q in range(PARTS):
            fetch(s, q).start()
    codes_copy.wait()
    codes = [scalar_ref[0, 64 + r * slots + s] for s in range(slots)]
    live = jnp.int32(0)
    for code in codes:
        live = live + present(code)
    chips = []
    for s, code in enumerate(codes):
        for coord, keep in ((coord_j(code), bs), (coord_k(code), cs)):
            chip = coord // (blocks * CORES)
            at = jnp.int32(0)
            for other in chips:
                at = at + (other == chip).astype(jnp.int32)
            chips.append(chip)
            at = jnp.where(present(code) > 0, at, 0)
            base = 0
            value = None
            for ref, capacity in zip(ins, CAPACITIES):
                if base >= 2 * s + 2:
                    break
                inside = (at >= base) & (at < base + capacity)
                held = ref[chip, jnp.where(inside, at - base, 0)].astype(F32)
                value = held if value is None else jnp.where(inside, held, value)
                base = base + capacity
            keep[s] = value.astype(keep.dtype)
    out_ref[...] = jnp.zeros_like(out_ref)

    def multiply(s, q):
        b = bs[s]
        c = cs[s]
        for a in range(q * part, (q + 1) * part, CHUNK):
            x = buf[s, a : a + CHUNK].reshape(CHUNK * edge, edge)
            inner = jnp.dot(x, c, preferred_element_type=F32).reshape(CHUNK, edge, edge)
            total = jnp.sum(inner * b[None], axis=1)
            for u in range(CHUNK // STRIP):
                out_ref[a // STRIP + u, s] = total[u * STRIP : (u + 1) * STRIP]

    def whole(s, carry):
        for q in range(PARTS):
            fetch(s, q).wait()
        for q in range(PARTS):
            multiply(s, q)
        return carry

    last = live - 1
    lax.fori_loop(0, last, whole, 0)

    @pl.when(live > 0)
    def _():
        for q in range(PARTS):
            fetch(last, q).wait()
            multiply(last, q)

    def drain(s, carry):
        for q in range(PARTS):
            fetch(s, q).wait()
        return carry

    lax.fori_loop(live, slots, drain, 0)


def eliminate(matrix):
    size = matrix.shape[0]
    down = lax.broadcasted_iota(jnp.int32, (size, size), 0)
    across = lax.broadcasted_iota(jnp.int32, (size, size), 1)
    eye = jnp.where(down == across, 1.0, 0.0).astype(F32)
    both = jnp.concatenate([matrix, eye], axis=1)
    below = lax.broadcasted_iota(jnp.int32, (size, 1), 0)
    for k in range(size):
        top = k // STRIP * STRIP
        rest = both[top:]
        row = both[k : k + 1]
        factor = rest[:, k : k + 1] * (1.0 / both[k : k + 1, k : k + 1])
        factor = jnp.where(below[top:] > k, factor, 0.0)
        rest = rest - factor * row
        both = rest if top == 0 else jnp.concatenate([both[:top], rest], axis=0)
    pivots = jnp.sum(jnp.where(down == across, both[:, :size], 0.0), axis=1, keepdims=True)
    return both[:, size:] * lax.rsqrt(pivots)


def times(a, b, over=((1,), (0,))):
    return lax.dot_general(a, b, (over, ((), ())), precision=HIGHEST, preferred_element_type=F32)


def factor_first(one_ref, other_ref, first_ref, side_ref, rest_ref):
    normal = one_ref[...] * other_ref[...]
    half = normal.shape[0] // 2
    first = eliminate(normal[:half, :half])
    side = times(normal[half:, :half], first, ((1,), (1,)))
    first_ref[...] = first
    side_ref[...] = side
    rest_ref[...] = normal[half:, half:] - times(side, side, ((1,), (1,)))


def factor_second(first_ref, side_ref, rest_ref, out_ref):
    first = first_ref[...]
    half = first.shape[0]
    second = eliminate(rest_ref[...])
    out_ref[:half, :half] = first
    out_ref[:half, half:] = jnp.zeros((half, half), F32)
    out_ref[half:, :half] = -times(times(second, side_ref[...]), first)
    out_ref[half:, half:] = second


def gather_blocks(code_ref, in_ref, out_ref, *, slots):
    out_ref[...] = jnp.zeros_like(out_ref)
    blocks = out_ref.shape[1]
    for d in range(in_ref.shape[0]):
        for s in range(slots):
            code = code_ref[0, d * slots + s]
            i = coord_i(code)
            value = jnp.where(present(code) > 0, in_ref[d, s], 0.0)
            out_ref[i // blocks, i % blocks] += value


def solve(in_ref, inv_ref, out_ref):
    total = in_ref[0]
    for q in range(1, in_ref.shape[0]):
        total = total + in_ref[q]
    blocks = total.shape[0]
    rows = total.reshape(blocks * STRIP, total.shape[2])
    inv = inv_ref[...]
    solved = times(times(rows, inv, ((1,), (1,))), inv).reshape(total.shape)
    largest = jnp.max(jnp.abs(solved), axis=2, keepdims=True)
    exponent = jnp.ceil(jnp.log2(jnp.maximum(largest, TINY)))
    scaled = solved * jnp.exp2(BITS - exponent)
    fixed = jnp.clip(jnp.round(scaled), 1 - FULL, FULL - 1).astype(jnp.int32).astype(jnp.int16)
    lane = lax.broadcasted_iota(jnp.int32, solved.shape[1:], 1)
    exponents = jnp.zeros(solved.shape[1:], F32)
    for b in range(blocks):
        exponents = jnp.where(lane == b, exponent[b], exponents)
    exponents = exponents.astype(jnp.int32).astype(jnp.int16)
    for d in range(out_ref.shape[0]):
        out_ref[d, :blocks] = fixed
        out_ref[d, blocks] = exponents


def unpack(in_ref, out_ref):
    blocks = out_ref.shape[0]
    for t in range(in_ref.shape[0]):
        scale = jnp.exp2(in_ref[t, blocks].astype(jnp.int32).astype(F32) - BITS)
        for b in range(blocks):
            out_ref[b, t] = in_ref[t, b].astype(jnp.int32).astype(F32) * scale[:, b : b + 1]


def body(tile_values, tile_coords, tile_owner, factor_b, factor_c):
    slots = tile_values.shape[0]
    edge = tile_values.shape[1]
    rank = factor_b.shape[1]
    shard = factor_b.shape[0]
    tiles_count = lax.axis_size("tiles")
    rows_count = lax.axis_size("rows")
    blocks = shard // edge
    tile = (STRIP, rank)
    half = (rank // 2, rank // 2)

    chips = rows_count // CORES

    def from_peer(x, peer):
        return lax.ppermute(x, "rows", [(q, peer(q)) for q in range(rows_count)])

    def swap(x):
        groups = [[x * CORES + core for x in range(chips)] for core in range(CORES)]
        return lax.all_to_all(x, "rows", 0, 0, axis_index_groups=groups, tiled=True)

    sibling_b, sibling_c = (from_peer(f, lambda q: q ^ 1) for f in (factor_b, factor_c))
    codes, rounds = pl.pallas_call(
        lambda *refs: plan(*refs, slots=slots, rows_count=rows_count, blocks=blocks),
        name="plan",
        out_shape=(
            jax.ShapeDtypeStruct((1, LANES), jnp.int32),
            jax.ShapeDtypeStruct((1, 1), jnp.int32),
        ),
        in_specs=[pl.BlockSpec(memory_space=pltpu.HBM)] * 2,
        out_specs=(vmem(), smem()),
        scratch_shapes=[
            pltpu.VMEM((1, tile_owner.shape[0]), jnp.int32),
            pltpu.VMEM((3, tile_owner.shape[0]), jnp.int32),
            pltpu.SemaphoreType.DMA((2,)),
        ],
        compiler_params=LIMIT,
    )(in_hbm(tile_owner.reshape(1, -1)), in_hbm(tile_coords.T))
    by_block = lambda f: f.reshape(blocks, edge, rank)
    sent = pl.pallas_call(
        lambda *refs: gather_factors(*refs, slots=slots),
        name="gather_factors",
        out_shape=tuple(jax.ShapeDtypeStruct((chips, c, edge, rank), BF16) for c in CAPACITIES),
        in_specs=[smem()] + [hbm()] * 4,
        out_specs=(vmem(),) * len(CAPACITIES),
        scratch_shapes=[pltpu.SemaphoreType.DMA],
        compiler_params=LIMIT,
    )(
        codes,
        in_hbm(by_block(factor_b)),
        in_hbm(by_block(factor_c)),
        by_block(sibling_b),
        by_block(sibling_c),
    )
    rest = lax.cond(rounds[0, 0] > 0, swap, lambda x: x, sent[1])
    first, rest = lax.optimization_barrier((sent[0], rest))
    chosen = [swap(first), rest]
    own_b, own_c, sibling_b, sibling_c, *sent = lax.optimization_barrier(
        (factor_b, factor_c, sibling_b, sibling_c, *sent)
    )
    gram = pl.pallas_call(
        chip_gram,
        name="chip_gram",
        out_shape=jax.ShapeDtypeStruct((rank, rank), F32),
        in_specs=[hbm()] * 4,
        out_specs=vmem(),
        scratch_shapes=[
            pltpu.VMEM((CORES, shard, rank), BF16),
            pltpu.SemaphoreType.DMA((CORES,)),
        ],
        compiler_params=LIMIT,
        cost_estimate=SMALL,
    )(in_hbm(own_b), in_hbm(own_c), sibling_b, sibling_c)
    away = [from_peer(gram, lambda q: (q + step) % rows_count) for step in range(CORES, rows_count, CORES)]
    gram = gram + sum(away[1:], away[0])
    chosen, gram = lax.optimization_barrier((chosen, gram))
    other = from_peer(gram, lambda q: q ^ 1)

    partials = pl.pallas_call(
        lambda *refs: contract(*refs, slots=slots, blocks=blocks),
        name="contract",
        out_shape=jax.ShapeDtypeStruct((tiles_count, slots) + tile, F32),
        in_specs=[vmem(), pl.BlockSpec(memory_space=pltpu.HBM)] + [vmem()] * len(CAPACITIES),
        out_specs=vmem(),
        scratch_shapes=[
            pltpu.VMEM(tile_values.shape, BF16),
            pltpu.VMEM((slots, edge, rank), F32),
            pltpu.VMEM((slots, edge, rank), BF16),
            pltpu.SMEM((1, LANES), jnp.int32),
            pltpu.SemaphoreType.DMA,
            pltpu.SemaphoreType.DMA((slots, PARTS)),
        ],
        compiler_params=pltpu.CompilerParams(vmem_limit_bytes=24 << 20),
        cost_estimate=pl.CostEstimate(flops=slots * 2 * edge**4, bytes_accessed=slots * 2 * edge**3, transcendentals=0),
    )(codes, in_hbm(tile_values), *chosen)
    moved = lax.all_to_all(partials, "tiles", 0, 0, tiled=True)
    halves = pl.pallas_call(
        factor_first,
        name="factor_first",
        out_shape=(jax.ShapeDtypeStruct(half, F32),) * 3,
        in_specs=[vmem()] * 2,
        out_specs=(vmem(),) * 3,
        compiler_params=LIMIT,
        cost_estimate=pl.CostEstimate(flops=1 << 30, bytes_accessed=1 << 20, transcendentals=64),
    )(gram, other)
    moved, halves = lax.optimization_barrier((moved, halves))
    dense = pl.pallas_call(
        lambda *refs: gather_blocks(*refs, slots=slots),
        name="gather_blocks",
        out_shape=jax.ShapeDtypeStruct((rows_count, blocks) + tile, F32),
        in_specs=[smem(), vmem()],
        out_specs=vmem(),
        compiler_params=LIMIT,
    )(codes, moved)
    owned = lax.all_to_all(dense, "rows", 0, 0, tiled=True)
    inverse = pl.pallas_call(
        factor_second,
        name="factor_second",
        out_shape=jax.ShapeDtypeStruct((rank, rank), F32),
        in_specs=[vmem()] * 3,
        out_specs=vmem(),
        compiler_params=LIMIT,
        cost_estimate=pl.CostEstimate(flops=1 << 30, bytes_accessed=1 << 20, transcendentals=64),
    )(*halves)
    solved = pl.pallas_call(
        solve,
        name="solve",
        out_shape=jax.ShapeDtypeStruct((tiles_count, blocks + 1) + tile, jnp.int16),
        in_specs=[vmem(), vmem()],
        out_specs=vmem(),
        compiler_params=LIMIT,
    )(owned, inverse)
    full = lax.all_to_all(solved, "tiles", 0, 0, tiled=True)
    out = pl.pallas_call(
        unpack,
        name="unpack",
        out_shape=jax.ShapeDtypeStruct((blocks, tiles_count) + tile, F32),
        in_specs=[vmem()],
        out_specs=vmem(),
        compiler_params=LIMIT,
    )(full)
    return out.reshape(shard, rank)


def solution(mesh):
    in_specs = (P(("tiles", "rows"), None, None, None), P(), P(), P("rows", None), P("rows", None))
    out_specs = P("rows", None)
    return jax.shard_map(body, mesh=mesh, in_specs=in_specs, out_specs=out_specs, check_vma=False)
```

time: 839 us -> 86.3 us (0.10)
  waiting for transfers between devices: 769 us -> 15.2 us
  Pallas kernels: 0 us -> 29.3 us
  other arithmetic: 27.2 us -> 0.02 us
  starting transfers between devices: 0.38 us -> 22.7 us
  local copies, waits for them, and re-layouts: 18.2 us -> 0.02 us
  blocking collectives: 0 us -> 17.6 us
  between operations: 13.3 us -> 0.76 us
  matrix products: 9.95 us -> 0 us
    reduce_scatter x1 -> x0, waiting for transfers between devices: 628 us -> none  [body(): lax.psum_scatter(summed.reshape(lax.axis_size(('tiles', 'rows')) * owned_...]
    all_gather x3 -> x0, waiting for transfers between devices: 94.2 us -> none  [the longest x1 36.5 us: body(): return lax.all_gather(solved, 'tiles', axis=0, tiled=True)]
    psum x1 -> x0, waiting for transfers between devices: 44.9 us -> none  [body(): lax.psum((factor_gram(factor_b), factor_gram(factor_c)), 'rows')]
    pallas_call x0 -> x9, Pallas kernels: none -> 29.3 us  [the longest x1 7.24 us: body(): pl.pallas_call(lambda *refs: contract(*refs, slots=slots, blocks=blocks),...]
    another operation x7 -> x0, other arithmetic: 23.2 us -> none  [the longest x3 12.4 us: body(): lower = jnp.linalg.cholesky(normal)]
    all_to_all x0 -> x1, blocking collectives: none -> 17.6 us  [body(): full = lax.all_to_all(solved, 'tiles', 0, 0, tiled=True)]
    all_to_all x0 -> x3, starting transfers between devices: none -> 17.1 us  [the longest x1 9.38 us: body(): moved = lax.all_to_all(partials, 'tiles', 0, 0, tiled=True)]
    ppermute x0 -> x6, waiting for transfers between devices: none -> 9.6 us  [from_peer(): return lax.ppermute(x, 'rows', [(q, peer(q)) for q in range(rows_count)])]
  transfers between devices with their start and end apart: 5 -> 9, of which waited for: 5 -> 6; matrix products, arithmetic and copies ran while one was open for 6% -> 0% of each run, Pallas kernels for 0% -> 18%
where the time goes in v2:
time: 86.3 us; the launch traced here: 85.7 us
  Pallas kernels  29.3 us (34%)
  starting transfers between devices  22.7 us (26%)
  blocking collectives  17.6 us (20%)
  waiting for transfers between devices  15.2 us (18%)
    all_to_all x1, blocking collectives, body(): full = lax.all_to_all(solved, 'tiles', 0, 0, tiled=True)  17.6 us
    ppermute x6, waiting for transfers between devices, from_peer(): return lax.ppermute(x, 'rows', [(q, peer(q)) for q in range(rows_count)])  9.6 us
    all_to_all x1, starting transfers between devices, body(): moved = lax.all_to_all(partials, 'tiles', 0, 0, tiled=True)  9.38 us
    pallas_call x1, Pallas kernels, body(): pl.pallas_call(lambda *refs: contract(*refs, slots=slots, blocks=blocks),...  7.24 us
    pallas_call x1, Pallas kernels, body(): pl.pallas_call(factor_first, name='factor_first', out_shape=(jax.ShapeDty...  6 us
    pallas_call x1, Pallas kernels, body(): pl.pallas_call(factor_second, name='factor_second', out_shape=jax.ShapeDt...  5.78 us
    ppermute x6, starting transfers between devices, from_peer(): return lax.ppermute(x, 'rows', [(q, peer(q)) for q in range(rows_count)])  5.61 us
    all_to_all x1, waiting for transfers between devices, body(): owned = lax.all_to_all(dense, 'rows', 0, 0, tiled=True)  4.47 us
  transfers between devices with their start and end apart: 9, of which 6 were waited for; matrix products, arithmetic and copies ran while one was open for 0% of the time, Pallas kernels for 18%

profile of v2, /device:TPU:0, one launch (start us, length us, event | category | flops | bytes accessed | tf_op | source)
XLA Modules:
  0.0 85.7 jit_solution(1460685600964769854)
XLA Ops:
  0.0 0.0 collective-permute-start
  0.0 0.5 collective-permute-start.1
  0.5 2.1 %plan.1 = (s32[1,128]{1,0:T(1,128)S(1)}, s32[1,1]{1,0:T(1,128)}) custom-call(s32[1,256]{1,0:T(1,128)} %bitcast.13, s32[3,256]{1,0:T(4,128)} %bitcast.12), custom_call_target="tpu_custom_call" | custom-call | tf_op jit(solution)/shard_map/plan/pallas_call | solution.py:344
  3.3 0.0 collective-permute-done.sb_ref
  3.3 0.0 collective-permute-done.1.sc_ref
  3.3 2.8 %gather_factors.1 = (bf16[4,6,128,128]{3,2,1,0:T(8,128)(2,1)}, bf16[4,2,128,128]{3,2,1,0:T(8,128)(2,1)S(1)}) custom-call(s32[1,128]{1,0:T(1,128)S(1)} %get-tuple-element.30.refs_0_, bf16[16,128,128]{2,1,0:T(8,128)(2,1)} %bitcast.10, bf16[16,128,128]{2,1,0:T(8,128)(2,1)} %bitcast.11, bf16[16,128,128]{2,1,0:T(8,128)(2,1)S(1)} %bitcast.8, ...), custom_call_target="tpu_custom_call" | custom-call | tf_op jit(solution)/shard_map/gather_factors/pallas_call | solution.py:361
  6.1 4.2 %all-to-all-start.1 = ((bf16[4,6,128,128]{3,2,1,0:T(8,128)(2,1)}), bf16[4,6,128,128]{3,2,1,0:T(8,128)(2,1)S(1)}, u32[]{:S(2)}, u32[]{:S(2)}) async-start(bf16[4,6,128,128]{3,2,1,0:T(8,128)(2,1)} %get-tuple-element.34), calls=%async_computation.1 | async-start | bytes 1572864 | tf_op jit(solution)/shard_map/all_to_all | solution.py:341
  10.4 1.5 %chip_gram.1 = f32[128,128]{1,0:T(8,128)S(1)} custom-call(bf16[2048,128]{1,0:T(8,128)(2,1)} %fb_ref, bf16[2048,128]{1,0:T(8,128)(2,1)} %fc_ref, bf16[2048,128]{1,0:T(8,128)(2,1)S(1)} %collective-permute-done.sb_ref, bf16[2048,128]{1,0:T(8,128)(2,1)S(1)} %collective-permute-done.1.sc_ref), custom_call_target="tpu_custom_call" | custom-call | flops 1024 | bytes 1024 | tf_op jit(solution)/shard_map/chip_gram/pallas_call | solution.py:382
  11.9 3.3 %collective-permute-start.4 = (f32[128,128]{1,0:T(8,128)S(1)}, f32[128,128]{1,0:T(8,128)S(1)}, u32[]{:S(2)}, u32[]{:S(2)}) collective-permute-start(f32[128,128]{1,0:T(8,128)S(1)} %chip_gram.1), channel_id=1, source_target_pairs={{0,6},{1,7},{2,0},{3,1},{4,2},{5,3},{6,4},{7,5},{8,14},{9,15},{10,... | collective-permute-start | bytes 196616 | tf_op jit(solution)/shard_map/ppermute | solution.py:337
  15.2 0.9 collective-permute-start.3
  16.1 0.9 %collective-permute-start.2 = (f32[128,128]{1,0:T(8,128)S(1)}, f32[128,128]{1,0:T(8,128)S(1)}, u32[]{:S(2)}, u32[]{:S(2)}) collective-permute-start(f32[128,128]{1,0:T(8,128)S(1)} %chip_gram.1), channel_id=1, source_target_pairs={{0,2},{1,3},{2,4},{3,5},{4,6},{5,7},{6,0},{7,1},{8,10},{9,11},{10,... | collective-permute-start | bytes 196616 | tf_op jit(solution)/shard_map/ppermute | solution.py:337
  16.9 6.5 %collective-permute-done.4 = f32[128,128]{1,0:T(8,128)S(1)} collective-permute-done((f32[128,128]{1,0:T(8,128)S(1)}, f32[128,128]{1,0:T(8,128)S(1)}, u32[]{:S(2)}, u32[]{:S(2)}) %collective-permute-start.4) | collective-permute-done | bytes 65568 | tf_op jit(solution)/shard_map/ppermute | solution.py:337
  23.4 1.6 %collective-permute-done.3 = f32[128,128]{1,0:T(8,128)S(1)} collective-permute-done((f32[128,128]{1,0:T(8,128)S(1)}, f32[128,128]{1,0:T(8,128)S(1)}, u32[]{:S(2)}, u32[]{:S(2)}) %collective-permute-start.3) | collective-permute-done | bytes 65568 | tf_op jit(solution)/shard_map/ppermute | solution.py:337
  25.0 0.3 collective-permute-done.2
  25.3 0.0 all-to-all-done.1.refs_2_
  25.3 7.2 %contract.1 = f32[16,4,8,128]{3,2,1,0:T(8,128)} custom-call(s32[1,128]{1,0:T(1,128)S(1)} %get-tuple-element.30.refs_0_, bf16[4,128,128,128]{3,2,1,0:T(8,128)(2,1)} %refs_1_.1, bf16[4,6,128,128]{3,2,1,0:T(8,128)(2,1)S(1)} %all-to-all-done.1.refs_2_, bf16[4,2,128,128]{3,2,1,0:T(8,128)(2,1)S(1)} %get-tuple-element.50.refs_3_), custom_call_target="tpu_custom_call" | custom-call | flops 2147483648 | bytes 16777216 | tf_op jit(solution)/shard_map/contract/pallas_call | solution.py:400
  32.6 9.4 %all-to-all-start.2 = ((f32[16,4,8,128]{3,2,1,0:T(8,128)}), f32[16,4,8,128]{3,2,1,0:T(8,128)S(1)}, u32[]{:S(2)}, u32[]{:S(2)}) async-start(f32[16,4,8,128]{3,2,1,0:T(8,128)} %contract.1), calls=%async_computation.2 | async-start | bytes 524288 | tf_op jit(solution)/shard_map/all_to_all | solution.py:417
  42.0 0.1 collective-permute-start.5
  42.1 1.2 %collective-permute-done.5.other_ref = f32[128,128]{1,0:T(8,128)S(1)} collective-permute-done((f32[128,128]{1,0:T(8,128)S(1)}, f32[128,128]{1,0:T(8,128)S(1)}, u32[]{:S(2)}, u32[]{:S(2)}) %collective-permute-start.5) | collective-permute-done | bytes 65568 | tf_op jit(solution)/shard_map/ppermute | solution.py:337
  43.3 6.0 %factor_first.1 = (f32[64,64]{1,0:T(8,128)S(1)}, f32[64,64]{1,0:T(8,128)S(1)}, f32[64,64]{1,0:T(8,128)S(1)}) custom-call(f32[128,128]{1,0:T(8,128)S(1)} %add_add_fusion.one_ref, f32[128,128]{1,0:T(8,128)S(1)} %collective-permute-done.5.other_ref), custom_call_target="tpu_custom_call" | custom-call | flops 1073741824 | bytes 1048576 | tf_op jit(solution)/shard_map/factor_first/pallas_call | solution.py:418
  49.3 1.1 %all-to-all-done.2.refs_1_ = f32[16,4,8,128]{3,2,1,0:T(8,128)S(1)} async-done(((f32[16,4,8,128]{3,2,1,0:T(8,128)}), f32[16,4,8,128]{3,2,1,0:T(8,128)S(1)}, u32[]{:S(2)}, u32[]{:S(2)}) %all-to-all-start.2) | async-done | bytes 262176 | tf_op jit(solution)/shard_map/all_to_all | solution.py:417
  50.4 1.7 %gather_blocks.1 = f32[8,16,8,128]{3,2,1,0:T(8,128)} custom-call(s32[1,128]{1,0:T(1,128)S(1)} %get-tuple-element.30.refs_0_, f32[16,4,8,128]{3,2,1,0:T(8,128)S(1)} %all-to-all-done.2.refs_1_), custom_call_target="tpu_custom_call" | custom-call | tf_op jit(solution)/shard_map/gather_blocks/pallas_call | solution.py:428
  52.2 3.5 %all-to-all-start.3 = ((f32[8,16,8,128]{3,2,1,0:T(8,128)}), f32[8,16,8,128]{3,2,1,0:T(8,128)S(1)}, u32[]{:S(2)}, u32[]{:S(2)}) async-start(f32[8,16,8,128]{3,2,1,0:T(8,128)} %gather_blocks.1), calls=%async_computation.3 | async-start | bytes 1048576 | tf_op jit(solution)/shard_map/all_to_all | solution.py:436
  55.7 5.8 %factor_second.1.inv_ref = f32[128,128]{1,0:T(8,128)S(1)} custom-call(f32[64,64]{1,0:T(8,128)S(1)} %get-tuple-element.47.first_ref, f32[64,64]{1,0:T(8,128)S(1)} %get-tuple-element.48.side_ref, f32[64,64]{1,0:T(8,128)S(1)} %get-tuple-element.49.rest_ref), custom_call_target="tpu_custom_call" | custom-call | flops 1073741824 | bytes 1048576 | tf_op jit(solution)/shard_map/factor_second/pallas_call | solution.py:437
  61.5 4.5 %all-to-all-done.3.in_ref = f32[8,16,8,128]{3,2,1,0:T(8,128)S(1)} async-done(((f32[8,16,8,128]{3,2,1,0:T(8,128)}), f32[8,16,8,128]{3,2,1,0:T(8,128)S(1)}, u32[]{:S(2)}, u32[]{:S(2)}) %all-to-all-start.3) | async-done | bytes 524320 | tf_op jit(solution)/shard_map/all_to_all | solution.py:436
  65.9 0.7 solve.1
  66.6 17.6 %all_to_all.25.in_ref = s16[16,17,8,128]{3,2,1,0:T(8,128)(2,1)S(1)} all-to-all(s16[16,17,8,128]{3,2,1,0:T(8,128)(2,1)S(1)} %solve.1), channel_id=1, replica_groups=mesh['tiles'=16,'rows'=8] {'tiles'}, dimensions={0} | all-to-all | bytes 1114112 | tf_op jit(solution)/shard_map/all_to_all | solution.py:454
  84.2 1.5 %unpack.1 = f32[16,16,8,128]{3,2,1,0:T(8,128)} custom-call(s16[16,17,8,128]{3,2,1,0:T(8,128)(2,1)S(1)} %all_to_all.25.in_ref), custom_call_target="tpu_custom_call" | custom-call | tf_op jit(solution)/shard_map/unpack/pallas_call | solution.py:455
  (3 shorter events, 0.1 us)
Async XLA Ops:
  0.0 3.3 %collective-permute-start = (bf16[2048,128]{1,0:T(8,128)(2,1)}, bf16[2048,128]{1,0:T(8,128)(2,1)S(1)}, u32[]{:S(2)}, u32[]{:S(2)}) collective-permute-start(bf16[2048,128]{1,0:T(8,128)(2,1)} %fb_ref), channel_id=1, source_target_pairs={{0,1},{1,0},{2,3},{3,2},{4,5},{5,4},{6,7},{7,6},{8,9},{9,8},{10,11... | collective-permute-start | bytes 1572872 | tf_op jit(solution)/shard_map/ppermute | solution.py:337
  0.0 3.3 %collective-permute-start.1 = (bf16[2048,128]{1,0:T(8,128)(2,1)}, bf16[2048,128]{1,0:T(8,128)(2,1)S(1)}, u32[]{:S(2)}, u32[]{:S(2)}) collective-permute-start(bf16[2048,128]{1,0:T(8,128)(2,1)} %fc_ref), channel_id=1, source_target_pairs={{0,1},{1,0},{2,3},{3,2},{4,5},{5,4},{6,7},{7,6},{8,9},{9,8},{10,11... | collective-permute-start | bytes 1572872 | tf_op jit(solution)/shard_map/ppermute | solution.py:337
  6.1 19.2 %all-to-all-start.1 = ((bf16[4,6,128,128]{3,2,1,0:T(8,128)(2,1)}), bf16[4,6,128,128]{3,2,1,0:T(8,128)(2,1)S(1)}, u32[]{:S(2)}, u32[]{:S(2)}) async-start(bf16[4,6,128,128]{3,2,1,0:T(8,128)(2,1)} %get-tuple-element.34), calls=%async_computation.1 | async-start | bytes 1572864 | tf_op jit(solution)/shard_map/all_to_all | solution.py:341
  11.9 11.5 %collective-permute-start.4 = (f32[128,128]{1,0:T(8,128)S(1)}, f32[128,128]{1,0:T(8,128)S(1)}, u32[]{:S(2)}, u32[]{:S(2)}) collective-permute-start(f32[128,128]{1,0:T(8,128)S(1)} %chip_gram.1), channel_id=1, source_target_pairs={{0,6},{1,7},{2,0},{3,1},{4,2},{5,3},{6,4},{7,5},{8,14},{9,15},{10,... | collective-permute-start | bytes 196616 | tf_op jit(solution)/shard_map/ppermute | solution.py:337
  15.2 9.8 %collective-permute-start.3 = (f32[128,128]{1,0:T(8,128)S(1)}, f32[128,128]{1,0:T(8,128)S(1)}, u32[]{:S(2)}, u32[]{:S(2)}) collective-permute-start(f32[128,128]{1,0:T(8,128)S(1)} %chip_gram.1), channel_id=1, source_target_pairs={{0,4},{1,5},{2,6},{3,7},{4,0},{5,1},{6,2},{7,3},{8,12},{9,13},{10,... | collective-permute-start | bytes 196616 | tf_op jit(solution)/shard_map/ppermute | solution.py:337
  16.1 9.2 %collective-permute-start.2 = (f32[128,128]{1,0:T(8,128)S(1)}, f32[128,128]{1,0:T(8,128)S(1)}, u32[]{:S(2)}, u32[]{:S(2)}) collective-permute-start(f32[128,128]{1,0:T(8,128)S(1)} %chip_gram.1), channel_id=1, source_target_pairs={{0,2},{1,3},{2,4},{3,5},{4,6},{5,7},{6,0},{7,1},{8,10},{9,11},{10,... | collective-permute-start | bytes 196616 | tf_op jit(solution)/shard_map/ppermute | solution.py:337
  32.6 17.9 %all-to-all-start.2 = ((f32[16,4,8,128]{3,2,1,0:T(8,128)}), f32[16,4,8,128]{3,2,1,0:T(8,128)S(1)}, u32[]{:S(2)}, u32[]{:S(2)}) async-start(f32[16,4,8,128]{3,2,1,0:T(8,128)} %contract.1), calls=%async_computation.2 | async-start | bytes 524288 | tf_op jit(solution)/shard_map/all_to_all | solution.py:417
  42.0 1.3 %collective-permute-start.5 = (f32[128,128]{1,0:T(8,128)S(1)}, f32[128,128]{1,0:T(8,128)S(1)}, u32[]{:S(2)}, u32[]{:S(2)}) collective-permute-start(f32[128,128]{1,0:T(8,128)S(1)} %add_add_fusion.one_ref), channel_id=1, source_target_pairs={{0,1},{1,0},{2,3},{3,2},{4,5},{5,4},{6,7},{7,6},{8,9},{9,8},{10,11... | collective-permute-start | bytes 196616 | tf_op jit(solution)/shard_map/ppermute | solution.py:337
  52.2 13.8 %all-to-all-start.3 = ((f32[8,16,8,128]{3,2,1,0:T(8,128)}), f32[8,16,8,128]{3,2,1,0:T(8,128)S(1)}, u32[]{:S(2)}, u32[]{:S(2)}) async-start(f32[8,16,8,128]{3,2,1,0:T(8,128)} %gather_blocks.1), calls=%async_computation.3 | async-start | bytes 1048576 | tf_op jit(solution)/shard_map/all_to_all | solution.py:436

commit v3 on v2

--- a/solution.py
+++ b/solution.py
@@ -115,20 +115,24 @@
             for own, sibling, coord in ((fb_ref, sb_ref, coord_j(code)), (fc_ref, sc_ref, coord_k(code))):
                 shard = coord // blocks
                 hit = (present(code) > 0) & (shard // CORES == r // CORES)
-                base = 0
-                for out, capacity in zip(outs, CAPACITIES):
-                    if base >= 2 * s + 2:
-                        break
-                    inside = hit & (at >= base) & (at < base + capacity)
-                    for ref, held in ((own, shard == r), (sibling, shard != r)):
-
-                        @pl.when(inside & held)
-                        def _(ref=ref, coord=coord, at=at, x=x, out=out, base=base):
-                            pltpu.make_async_copy(
-                                ref.at[coord % blocks], out.at[x, at - base], sem
-                            ).start()
-
-                    base = base + capacity
+
+                @pl.when(hit)
+                def _(own=own, sibling=sibling, coord=coord, shard=shard, at=at, x=x, s=s):
+                    base = 0
+                    for out, capacity in zip(outs, CAPACITIES):
+                        if base >= 2 * s + 2:
+                            break
+                        inside = (at >= base) & (at < base + capacity)
+                        for ref, held in ((own, shard == r), (sibling, shard != r)):
+
+                            @pl.when(inside & held)
+                            def _(ref=ref, out=out, base=base):
+                                pltpu.make_async_copy(
+                                    ref.at[coord % blocks], out.at[x, at - base], sem
+                                ).start()
+
+                        base = base + capacity
+
                 at = at + hit.astype(jnp.int32)
         count = count + at
 
@@ -242,14 +246,43 @@
     across = lax.broadcasted_iota(jnp.int32, (size, size), 1)
     eye = jnp.where(down == across, 1.0, 0.0).astype(F32)
     both = jnp.concatenate([matrix, eye], axis=1)
-    below = lax.broadcasted_iota(jnp.int32, (size, 1), 0)
-    for k in range(size):
+    wide = lax.broadcasted_iota(jnp.int32, both.shape, 0)
+
+    def spread(x):
+        return jnp.broadcast_to(x, (x.shape[0], both.shape[1]))
+
+    def pair(p, q, r):
+        over = 1.0 / p
+        ratio = q * over
+        low = 1.0 / (r - q * ratio)
+        side = ratio * low
+        return over + ratio * side, side, low, ratio
+
+    for k in range(0, size, 4):
         top = k // STRIP * STRIP
         rest = both[top:]
-        row = both[k : k + 1]
-        factor = rest[:, k : k + 1] * (1.0 / both[k : k + 1, k : k + 1])
-        factor = jnp.where(below[top:] > k, factor, 0.0)
-        rest = rest - factor * row
+        row = [both[k + i : k + i + 1] for i in range(4)]
+        p = {(i, j): spread(row[i][:, k + j : k + j + 1]) for i in range(4) for j in range(i, 4)}
+        col = [spread(rest[:, k + j : k + j + 1]) for j in range(4)]
+        a, b, c, ratio = pair(p[0, 0], p[0, 1], p[1, 1])
+        u0, u1 = a * row[0] - b * row[1], c * row[1] - b * row[0]
+        u02, u12 = a * p[0, 2] - b * p[1, 2], c * p[1, 2] - b * p[0, 2]
+        u03, u13 = a * p[0, 3] - b * p[1, 3], c * p[1, 3] - b * p[0, 3]
+        row2 = row[2] - p[0, 2] * u0 - p[1, 2] * u1
+        row3 = row[3] - p[0, 3] * u0 - p[1, 3] * u1
+        s22 = p[2, 2] - p[0, 2] * u02 - p[1, 2] * u12
+        s23 = p[2, 3] - p[0, 3] * u02 - p[1, 3] * u12
+        s33 = p[3, 3] - p[0, 3] * u03 - p[1, 3] * u13
+        a, b, c, ratio2 = pair(s22, s23, s33)
+        u2, u3 = a * row2 - b * row3, c * row3 - b * row2
+        v0 = u0 - u02 * u2 - u03 * u3
+        v1 = u1 - u12 * u2 - u13 * u3
+        at = wide[top:]
+        later = rest - col[0] * v0 - col[1] * v1 - col[2] * u2 - col[3] * u3
+        rest = jnp.where(at == k + 1, row[1] - ratio * row[0], rest)
+        rest = jnp.where(at == k + 2, row2, rest)
+        rest = jnp.where(at == k + 3, row3 - ratio2 * row2, rest)
+        rest = jnp.where(at > k + 3, later, rest)
         both = rest if top == 0 else jnp.concatenate([both[:top], rest], axis=0)
     pivots = jnp.sum(jnp.where(down == across, both[:, :size], 0.0), axis=1, keepdims=True)
     return both[:, size:] * lax.rsqrt(pivots)
@@ -259,23 +292,15 @@
     return lax.dot_general(a, b, (over, ((), ())), precision=HIGHEST, preferred_element_type=F32)
 
 
-def factor_first(one_ref, other_ref, first_ref, side_ref, rest_ref):
+def invert(one_ref, other_ref, out_ref):
     normal = one_ref[...] * other_ref[...]
     half = normal.shape[0] // 2
     first = eliminate(normal[:half, :half])
     side = times(normal[half:, :half], first, ((1,), (1,)))
-    first_ref[...] = first
-    side_ref[...] = side
-    rest_ref[...] = normal[half:, half:] - times(side, side, ((1,), (1,)))
-
-
-def factor_second(first_ref, side_ref, rest_ref, out_ref):
-    first = first_ref[...]
-    half = first.shape[0]
-    second = eliminate(rest_ref[...])
+    second = eliminate(normal[half:, half:] - times(side, side, ((1,), (1,))))
     out_ref[:half, :half] = first
     out_ref[:half, half:] = jnp.zeros((half, half), F32)
-    out_ref[half:, :half] = -times(times(second, side_ref[...]), first)
+    out_ref[half:, :half] = -times(second, times(side, first))
     out_ref[half:, half:] = second
 
 
@@ -329,7 +354,6 @@
     rows_count = lax.axis_size("rows")
     blocks = shard // edge
     tile = (STRIP, rank)
-    half = (rank // 2, rank // 2)
 
     chips = rows_count // CORES
 
@@ -392,10 +416,8 @@
         compiler_params=LIMIT,
         cost_estimate=SMALL,
     )(in_hbm(own_b), in_hbm(own_c), sibling_b, sibling_c)
-    away = [from_peer(gram, lambda q: (q + step) % rows_count) for step in range(CORES, rows_count, CORES)]
-    gram = gram + sum(away[1:], away[0])
+    gram = gram + from_peer(gram, lambda q: q ^ CORES)
     chosen, gram = lax.optimization_barrier((chosen, gram))
-    other = from_peer(gram, lambda q: q ^ 1)
 
     partials = pl.pallas_call(
         lambda *refs: contract(*refs, slots=slots, blocks=blocks),
@@ -415,16 +437,8 @@
         cost_estimate=pl.CostEstimate(flops=slots * 2 * edge**4, bytes_accessed=slots * 2 * edge**3, transcendentals=0),
     )(codes, in_hbm(tile_values), *chosen)
     moved = lax.all_to_all(partials, "tiles", 0, 0, tiled=True)
-    halves = pl.pallas_call(
-        factor_first,
-        name="factor_first",
-        out_shape=(jax.ShapeDtypeStruct(half, F32),) * 3,
-        in_specs=[vmem()] * 2,
-        out_specs=(vmem(),) * 3,
-        compiler_params=LIMIT,
-        cost_estimate=pl.CostEstimate(flops=1 << 30, bytes_accessed=1 << 20, transcendentals=64),
-    )(gram, other)
-    moved, halves = lax.optimization_barrier((moved, halves))
+    gram = gram + from_peer(gram, lambda q: (chips - 1 - q // CORES) * CORES + q % CORES)
+    moved, gram = lax.optimization_barrier((moved, gram))
     dense = pl.pallas_call(
         lambda *refs: gather_blocks(*refs, slots=slots),
         name="gather_blocks",
@@ -433,16 +447,18 @@
         out_specs=vmem(),
         compiler_params=LIMIT,
     )(codes, moved)
+    dense, gram = lax.optimization_barrier((dense, gram))
+    other = from_peer(gram, lambda q: q ^ 1)
     owned = lax.all_to_all(dense, "rows", 0, 0, tiled=True)
     inverse = pl.pallas_call(
-        factor_second,
-        name="factor_second",
+        invert,
+        name="invert",
         out_shape=jax.ShapeDtypeStruct((rank, rank), F32),
-        in_specs=[vmem()] * 3,
+        in_specs=[vmem()] * 2,
         out_specs=vmem(),
         compiler_params=LIMIT,
         cost_estimate=pl.CostEstimate(flops=1 << 30, bytes_accessed=1 << 20, transcendentals=64),
-    )(*halves)
+    )(gram, other)
     solved = pl.pallas_call(
         solve,
         name="solve",

time: 86.3 us -> 82.5 us (0.956)
  Pallas kernels: 29.3 us -> 23.1 us
  waiting for transfers between devices: 15.2 us -> 20 us
  blocking collectives: 17.6 us -> 15.9 us
    pallas_call x2 -> x1, Pallas kernels: 11.8 us -> 6.18 us  [body(): pl.pallas_call(invert, name='invert', out_shape=jax.ShapeDtypeStruct((ran...]
    ppermute x6 -> x5, waiting for transfers between devices: 9.6 us -> 13.5 us  [from_peer(): return lax.ppermute(x, 'rows', [(q, peer(q)) for q in range(rows_count)])]
    all_to_all x1, blocking collectives: 17.6 us -> 15.9 us  [body(): full = lax.all_to_all(solved, 'tiles', 0, 0, tiled=True)]
    all_to_all x1, waiting for transfers between devices: 1.13 us -> 2.9 us  [body(): moved = lax.all_to_all(partials, 'tiles', 0, 0, tiled=True)]
    all_to_all x1, waiting for transfers between devices: 4.47 us -> 2.75 us  [body(): owned = lax.all_to_all(dense, 'rows', 0, 0, tiled=True)]
    ppermute x6 -> x5, starting transfers between devices: 5.61 us -> 4.5 us  [from_peer(): return lax.ppermute(x, 'rows', [(q, peer(q)) for q in range(rows_count)])]
  transfers between devices with their start and end apart: 9 -> 8, of which waited for: 6 -> 6; matrix products, arithmetic and copies ran while one was open for 0% -> 0% of each run, Pallas kernels for 18% -> 12%
where the time goes in v3:
time: 82.5 us; the launch traced here: 81.8 us
  Pallas kernels  23.1 us (28%)
  starting transfers between devices  22.1 us (27%)
  waiting for transfers between devices  20 us (24%)
  blocking collectives  15.9 us (19%)
    all_to_all x1, blocking collectives, body(): full = lax.all_to_all(solved, 'tiles', 0, 0, tiled=True)  15.9 us
    ppermute x5, waiting for transfers between devices, from_peer(): return lax.ppermute(x, 'rows', [(q, peer(q)) for q in range(rows_count)])  13.5 us
    all_to_all x1, starting transfers between devices, body(): moved = lax.all_to_all(partials, 'tiles', 0, 0, tiled=True)  9.93 us
    pallas_call x1, Pallas kernels, body(): pl.pallas_call(lambda *refs: contract(*refs, slots=slots, blocks=blocks),...  6.64 us
    pallas_call x1, Pallas kernels, body(): pl.pallas_call(invert, name='invert', out_shape=jax.ShapeDtypeStruct((ran...  6.18 us
    ppermute x5, starting transfers between devices, from_peer(): return lax.ppermute(x, 'rows', [(q, peer(q)) for q in range(rows_count)])  4.5 us
    all_to_all x1, starting transfers between devices, swap(): return lax.all_to_all(x, 'rows', 0, 0, axis_index_groups=groups, tiled=True)  4.16 us
    all_to_all x1, starting transfers between devices, body(): owned = lax.all_to_all(dense, 'rows', 0, 0, tiled=True)  3.49 us
  transfers between devices with their start and end apart: 8, of which 6 were waited for; matrix products, arithmetic and copies ran while one was open for 0% of the time, Pallas kernels for 12%

profile of v3, /device:TPU:0, one launch (start us, length us, event | category | flops | bytes accessed | tf_op | source)
XLA Modules:
  0.0 81.8 jit_solution(17729089309774437559)
XLA Ops:
  0.0 0.0 collective-permute-start
  0.0 0.5 collective-permute-start.1
  0.5 2.1 %plan.1 = (s32[1,128]{1,0:T(1,128)S(1)}, s32[1,1]{1,0:T(1,128)}) custom-call(s32[1,256]{1,0:T(1,128)} %bitcast.13, s32[3,256]{1,0:T(4,128)} %bitcast.12), custom_call_target="tpu_custom_call" | custom-call | tf_op jit(solution)/shard_map/plan/pallas_call | solution.py:368
  3.3 0.0 collective-permute-done.sb_ref
  3.3 0.0 collective-permute-done.1.sc_ref
  3.3 2.8 %gather_factors.1 = (bf16[4,6,128,128]{3,2,1,0:T(8,128)(2,1)}, bf16[4,2,128,128]{3,2,1,0:T(8,128)(2,1)S(1)}) custom-call(s32[1,128]{1,0:T(1,128)S(1)} %get-tuple-element.27.refs_0_, bf16[16,128,128]{2,1,0:T(8,128)(2,1)} %bitcast.10, bf16[16,128,128]{2,1,0:T(8,128)(2,1)} %bitcast.11, bf16[16,128,128]{2,1,0:T(8,128)(2,1)S(1)} %bitcast.8, ...), custom_call_target="tpu_custom_call" | custom-call | tf_op jit(solution)/shard_map/gather_factors/pallas_call | solution.py:385
  6.2 4.2 %all-to-all-start.1 = ((bf16[4,6,128,128]{3,2,1,0:T(8,128)(2,1)}), bf16[4,6,128,128]{3,2,1,0:T(8,128)(2,1)S(1)}, u32[]{:S(2)}, u32[]{:S(2)}) async-start(bf16[4,6,128,128]{3,2,1,0:T(8,128)(2,1)} %get-tuple-element.31), calls=%async_computation.1 | async-start | bytes 1572864 | tf_op jit(solution)/shard_map/all_to_all | solution.py:365
  10.3 1.5 %chip_gram.1 = f32[128,128]{1,0:T(8,128)S(1)} custom-call(bf16[2048,128]{1,0:T(8,128)(2,1)} %fb_ref, bf16[2048,128]{1,0:T(8,128)(2,1)} %fc_ref, bf16[2048,128]{1,0:T(8,128)(2,1)S(1)} %collective-permute-done.sb_ref, bf16[2048,128]{1,0:T(8,128)(2,1)S(1)} %collective-permute-done.1.sc_ref), custom_call_target="tpu_custom_call" | custom-call | flops 1024 | bytes 1024 | tf_op jit(solution)/shard_map/chip_gram/pallas_call | solution.py:406
  11.9 2.1 %collective-permute-start.2 = (f32[128,128]{1,0:T(8,128)S(1)}, f32[128,128]{1,0:T(8,128)S(1)}, u32[]{:S(2)}, u32[]{:S(2)}) collective-permute-start(f32[128,128]{1,0:T(8,128)S(1)} %chip_gram.1), channel_id=1, source_target_pairs={{0,2},{1,3},{2,0},{3,1},{4,6},{5,7},{6,4},{7,5},{8,10},{9,11},{10,... | collective-permute-start | bytes 196616 | tf_op jit(solution)/shard_map/ppermute | solution.py:361
  14.0 8.5 %collective-permute-done.2 = f32[128,128]{1,0:T(8,128)S(1)} collective-permute-done((f32[128,128]{1,0:T(8,128)S(1)}, f32[128,128]{1,0:T(8,128)S(1)}, u32[]{:S(2)}, u32[]{:S(2)}) %collective-permute-start.2) | collective-permute-done | bytes 65568 | tf_op jit(solution)/shard_map/ppermute | solution.py:361
  22.5 0.8 all-to-all-done.1.refs_2_
  23.3 6.6 %contract.1 = f32[16,4,8,128]{3,2,1,0:T(8,128)} custom-call(s32[1,128]{1,0:T(1,128)S(1)} %get-tuple-element.27.refs_0_, bf16[4,128,128,128]{3,2,1,0:T(8,128)(2,1)} %refs_1_.1, bf16[4,6,128,128]{3,2,1,0:T(8,128)(2,1)S(1)} %all-to-all-done.1.refs_2_, bf16[4,2,128,128]{3,2,1,0:T(8,128)(2,1)S(1)} %get-tuple-element.44.refs_3_), custom_call_target="tpu_custom_call" | custom-call | flops 2147483648 | bytes 16777216 | tf_op jit(solution)/shard_map/contract/pallas_call | solution.py:422
  29.9 9.9 %all-to-all-start.2 = ((f32[16,4,8,128]{3,2,1,0:T(8,128)}), f32[16,4,8,128]{3,2,1,0:T(8,128)S(1)}, u32[]{:S(2)}, u32[]{:S(2)}) async-start(f32[16,4,8,128]{3,2,1,0:T(8,128)} %contract.1), calls=%async_computation.2 | async-start | bytes 524288 | tf_op jit(solution)/shard_map/all_to_all | solution.py:439
  39.9 1.5 %collective-permute-start.3 = (f32[128,128]{1,0:T(8,128)S(1)}, f32[128,128]{1,0:T(8,128)S(1)}, u32[]{:S(2)}, u32[]{:S(2)}) collective-permute-start(f32[128,128]{1,0:T(8,128)S(1)} %add.6), channel_id=1, source_target_pairs={{0,6},{1,7},{2,4},{3,5},{4,2},{5,3},{6,0},{7,1},{8,14},{9,15},{10,... | collective-permute-start | bytes 196616 | tf_op jit(solution)/shard_map/ppermute | solution.py:361
  41.4 4.1 %collective-permute-done.3 = f32[128,128]{1,0:T(8,128)S(1)} collective-permute-done((f32[128,128]{1,0:T(8,128)S(1)}, f32[128,128]{1,0:T(8,128)S(1)}, u32[]{:S(2)}, u32[]{:S(2)}) %collective-permute-start.3) | collective-permute-done | bytes 65568 | tf_op jit(solution)/shard_map/ppermute | solution.py:361
  45.4 2.9 %all-to-all-done.2.refs_1_ = f32[16,4,8,128]{3,2,1,0:T(8,128)S(1)} async-done(((f32[16,4,8,128]{3,2,1,0:T(8,128)}), f32[16,4,8,128]{3,2,1,0:T(8,128)S(1)}, u32[]{:S(2)}, u32[]{:S(2)}) %all-to-all-start.2) | async-done | bytes 262176 | tf_op jit(solution)/shard_map/all_to_all | solution.py:439
  48.3 1.7 %gather_blocks.1 = f32[8,16,8,128]{3,2,1,0:T(8,128)} custom-call(s32[1,128]{1,0:T(1,128)S(1)} %get-tuple-element.27.refs_0_, f32[16,4,8,128]{3,2,1,0:T(8,128)S(1)} %all-to-all-done.2.refs_1_), custom_call_target="tpu_custom_call" | custom-call | tf_op jit(solution)/shard_map/gather_blocks/pallas_call | solution.py:442
  50.1 3.5 %all-to-all-start.3 = ((f32[8,16,8,128]{3,2,1,0:T(8,128)}), f32[8,16,8,128]{3,2,1,0:T(8,128)S(1)}, u32[]{:S(2)}, u32[]{:S(2)}) async-start(f32[8,16,8,128]{3,2,1,0:T(8,128)} %gather_blocks.1), calls=%async_computation.3 | async-start | bytes 1048576 | tf_op jit(solution)/shard_map/all_to_all | solution.py:452
  53.6 0.4 collective-permute-start.4
  54.0 0.9 %collective-permute-done.4.other_ref = f32[128,128]{1,0:T(8,128)S(1)} collective-permute-done((f32[128,128]{1,0:T(8,128)S(1)}, f32[128,128]{1,0:T(8,128)S(1)}, u32[]{:S(2)}, u32[]{:S(2)}) %collective-permute-start.4) | collective-permute-done | bytes 65568 | tf_op jit(solution)/shard_map/ppermute | solution.py:361
  54.9 6.2 %invert.1.inv_ref = f32[128,128]{1,0:T(8,128)S(1)} custom-call(f32[128,128]{1,0:T(8,128)S(1)} %add.7.one_ref, f32[128,128]{1,0:T(8,128)S(1)} %collective-permute-done.4.other_ref), custom_call_target="tpu_custom_call" | custom-call | flops 1073741824 | bytes 1048576 | tf_op jit(solution)/shard_map/invert/pallas_call | solution.py:453
  61.1 2.7 %all-to-all-done.3.in_ref = f32[8,16,8,128]{3,2,1,0:T(8,128)S(1)} async-done(((f32[8,16,8,128]{3,2,1,0:T(8,128)}), f32[8,16,8,128]{3,2,1,0:T(8,128)S(1)}, u32[]{:S(2)}, u32[]{:S(2)}) %all-to-all-start.3) | async-done | bytes 524320 | tf_op jit(solution)/shard_map/all_to_all | solution.py:452
  63.8 0.7 solve.1
  64.5 15.9 %all_to_all.25.in_ref = s16[16,17,8,128]{3,2,1,0:T(8,128)(2,1)S(1)} all-to-all(s16[16,17,8,128]{3,2,1,0:T(8,128)(2,1)S(1)} %solve.1), channel_id=1, replica_groups=mesh['tiles'=16,'rows'=8] {'tiles'}, dimensions={0} | all-to-all | bytes 1114112 | tf_op jit(solution)/shard_map/all_to_all | solution.py:470
  80.4 1.5 %unpack.1 = f32[16,16,8,128]{3,2,1,0:T(8,128)} custom-call(s16[16,17,8,128]{3,2,1,0:T(8,128)(2,1)S(1)} %all_to_all.25.in_ref), custom_call_target="tpu_custom_call" | custom-call | tf_op jit(solution)/shard_map/unpack/pallas_call | solution.py:471
  (4 shorter events, 0.1 us)
Async XLA Ops:
  0.0 3.3 %collective-permute-start = (bf16[2048,128]{1,0:T(8,128)(2,1)}, bf16[2048,128]{1,0:T(8,128)(2,1)S(1)}, u32[]{:S(2)}, u32[]{:S(2)}) collective-permute-start(bf16[2048,128]{1,0:T(8,128)(2,1)} %fb_ref), channel_id=1, source_target_pairs={{0,1},{1,0},{2,3},{3,2},{4,5},{5,4},{6,7},{7,6},{8,9},{9,8},{10,11... | collective-permute-start | bytes 1572872 | tf_op jit(solution)/shard_map/ppermute | solution.py:361
  0.0 3.3 %collective-permute-start.1 = (bf16[2048,128]{1,0:T(8,128)(2,1)}, bf16[2048,128]{1,0:T(8,128)(2,1)S(1)}, u32[]{:S(2)}, u32[]{:S(2)}) collective-permute-start(bf16[2048,128]{1,0:T(8,128)(2,1)} %fc_ref), channel_id=1, source_target_pairs={{0,1},{1,0},{2,3},{3,2},{4,5},{5,4},{6,7},{7,6},{8,9},{9,8},{10,11... | collective-permute-start | bytes 1572872 | tf_op jit(solution)/shard_map/ppermute | solution.py:361
  6.2 17.1 %all-to-all-start.1 = ((bf16[4,6,128,128]{3,2,1,0:T(8,128)(2,1)}), bf16[4,6,128,128]{3,2,1,0:T(8,128)(2,1)S(1)}, u32[]{:S(2)}, u32[]{:S(2)}) async-start(bf16[4,6,128,128]{3,2,1,0:T(8,128)(2,1)} %get-tuple-element.31), calls=%async_computation.1 | async-start | bytes 1572864 | tf_op jit(solution)/shard_map/all_to_all | solution.py:365
  11.9 10.6 %collective-permute-start.2 = (f32[128,128]{1,0:T(8,128)S(1)}, f32[128,128]{1,0:T(8,128)S(1)}, u32[]{:S(2)}, u32[]{:S(2)}) collective-permute-start(f32[128,128]{1,0:T(8,128)S(1)} %chip_gram.1), channel_id=1, source_target_pairs={{0,2},{1,3},{2,0},{3,1},{4,6},{5,7},{6,4},{7,5},{8,10},{9,11},{10,... | collective-permute-start | bytes 196616 | tf_op jit(solution)/shard_map/ppermute | solution.py:361
  29.9 18.4 %all-to-all-start.2 = ((f32[16,4,8,128]{3,2,1,0:T(8,128)}), f32[16,4,8,128]{3,2,1,0:T(8,128)S(1)}, u32[]{:S(2)}, u32[]{:S(2)}) async-start(f32[16,4,8,128]{3,2,1,0:T(8,128)} %contract.1), calls=%async_computation.2 | async-start | bytes 524288 | tf_op jit(solution)/shard_map/all_to_all | solution.py:439
  39.9 5.6 %collective-permute-start.3 = (f32[128,128]{1,0:T(8,128)S(1)}, f32[128,128]{1,0:T(8,128)S(1)}, u32[]{:S(2)}, u32[]{:S(2)}) collective-permute-start(f32[128,128]{1,0:T(8,128)S(1)} %add.6), channel_id=1, source_target_pairs={{0,6},{1,7},{2,4},{3,5},{4,2},{5,3},{6,0},{7,1},{8,14},{9,15},{10,... | collective-permute-start | bytes 196616 | tf_op jit(solution)/shard_map/ppermute | solution.py:361
  50.1 13.8 %all-to-all-start.3 = ((f32[8,16,8,128]{3,2,1,0:T(8,128)}), f32[8,16,8,128]{3,2,1,0:T(8,128)S(1)}, u32[]{:S(2)}, u32[]{:S(2)}) async-start(f32[8,16,8,128]{3,2,1,0:T(8,128)} %gather_blocks.1), calls=%async_computation.3 | async-start | bytes 1048576 | tf_op jit(solution)/shard_map/all_to_all | solution.py:452
  53.6 1.3 %collective-permute-start.4 = (f32[128,128]{1,0:T(8,128)S(1)}, f32[128,128]{1,0:T(8,128)S(1)}, u32[]{:S(2)}, u32[]{:S(2)}) collective-permute-start(f32[128,128]{1,0:T(8,128)S(1)} %add.7.one_ref), channel_id=1, source_target_pairs={{0,1},{1,0},{2,3},{3,2},{4,5},{5,4},{6,7},{7,6},{8,9},{9,8},{10,11... | collective-permute-start | bytes 196616 | tf_op jit(solution)/shard_map/ppermute | solution.py:361

commit v4 on v3

--- a/solution.py
+++ b/solution.py
@@ -54,7 +54,10 @@
     return code >> PRESENT
 
 
-def plan(owner_hbm, coords_hbm, code_ref, rounds_ref, owner_ref, coords_ref, sem, *, slots, rows_count, blocks):
+def plan(
+    owner_hbm, coords_hbm, fb_hbm, fc_hbm, code_ref, rounds_ref, fb_ref, fc_ref, owner_ref, coords_ref, sem,
+    *, slots, rows_count, blocks
+):
     t = lax.axis_index("tiles")
     r = lax.axis_index("rows")
     tiles = owner_ref.shape[1]
@@ -64,7 +67,11 @@
         pltpu.make_async_copy(owner_hbm, owner_ref, sem.at[0]),
         pltpu.make_async_copy(coords_hbm, coords_ref, sem.at[1]),
     ]
-    for load in loads:
+    shards = [
+        pltpu.make_async_copy(fb_hbm, fb_ref, sem.at[2]),
+        pltpu.make_async_copy(fc_hbm, fc_ref, sem.at[3]),
+    ]
+    for load in loads + shards:
         load.start()
     for load in loads:
         load.wait()
@@ -101,6 +108,8 @@
         base = base + capacity
         rounds = rounds + jnp.where(most > base, 1, 0)
     rounds_ref[0, 0] = jnp.sum(rounds)
+    for load in shards:
+        load.wait()
 
 
 def gather_factors(code_ref, fb_ref, fc_ref, sb_ref, sc_ref, *refs, slots):
@@ -164,7 +173,13 @@
     )
 
 
-def contract(code_ref, x_ref, *refs, slots, blocks):
+def load_part(x_ref, out_ref, sem):
+    copy = pltpu.make_async_copy(x_ref.at[0, pl.ds(0, out_ref.shape[0])], out_ref, sem)
+    copy.start()
+    copy.wait()
+
+
+def contract(code_ref, x_ref, part_ref, *refs, slots, blocks):
     ins = refs[: len(CAPACITIES)]
     out_ref, buf, bs, cs, scalar_ref, code_sem, sem = refs[len(CAPACITIES) :]
     r = lax.axis_index("rows")
@@ -177,8 +192,12 @@
 
     codes_copy = pltpu.make_async_copy(code_ref, scalar_ref, code_sem)
     codes_copy.start()
+    early = part_ref.shape[0] // part
+    for q in range(early):
+        rows = pl.ds(q * part, part)
+        pltpu.make_async_copy(part_ref.at[rows], buf.at[0, rows], sem.at[0, q]).start()
     for s in range(slots):
-        for q in range(PARTS):
+        for q in range(early if s == 0 else 0, PARTS):
             fetch(s, q).start()
     codes_copy.wait()
     codes = [scalar_ref[0, 64 + r * slots + s] for s in range(slots)]
@@ -304,15 +323,19 @@
     out_ref[half:, half:] = second
 
 
-def gather_blocks(code_ref, in_ref, out_ref, *, slots):
-    out_ref[...] = jnp.zeros_like(out_ref)
-    blocks = out_ref.shape[1]
+def gather_blocks(code_ref, in_ref, keep_ref, send_ref, both, *, slots):
+    core = lax.axis_index("rows") % CORES
+    blocks = both.shape[2]
+    both[...] = jnp.zeros_like(both)
     for d in range(in_ref.shape[0]):
         for s in range(slots):
             code = code_ref[0, d * slots + s]
             i = coord_i(code)
+            shard = i // blocks
             value = jnp.where(present(code) > 0, in_ref[d, s], 0.0)
-            out_ref[i // blocks, i % blocks] += value
+            both[(shard + core) % CORES, shard // CORES, i % blocks] += value
+    keep_ref[...] = both[0]
+    send_ref[...] = both[1]
 
 
 def solve(in_ref, inv_ref, out_ref):
@@ -337,12 +360,22 @@
         out_ref[d, blocks] = exponents
 
 
-def unpack(in_ref, out_ref):
+def unpack(in_ref, out_ref, buf, sem):
     blocks = out_ref.shape[0]
+    group = blocks // sem.shape[0]
+    scales = []
     for t in range(in_ref.shape[0]):
-        scale = jnp.exp2(in_ref[t, blocks].astype(jnp.int32).astype(F32) - BITS)
-        for b in range(blocks):
-            out_ref[b, t] = in_ref[t, b].astype(jnp.int32).astype(F32) * scale[:, b : b + 1]
+        scales.append(jnp.exp2(in_ref[t, blocks].astype(jnp.int32).astype(F32) - BITS))
+    copies = []
+    for g in range(sem.shape[0]):
+        for b in range(g * group, (g + 1) * group):
+            for t, scale in enumerate(scales):
+                buf[b, t] = in_ref[t, b].astype(jnp.int32).astype(F32) * scale[:, b : b + 1]
+        part = pl.ds(g * group, group)
+        copies.append(pltpu.make_async_copy(buf.at[part], out_ref.at[part], sem.at[g]))
+        copies[-1].start()
+    for copy in copies:
+        copy.wait()
 
 
 def body(tile_values, tile_coords, tile_owner, factor_b, factor_c):
@@ -365,43 +398,51 @@
         return lax.all_to_all(x, "rows", 0, 0, axis_index_groups=groups, tiled=True)
 
     sibling_b, sibling_c = (from_peer(f, lambda q: q ^ 1) for f in (factor_b, factor_c))
-    codes, rounds = pl.pallas_call(
+    by_block = lambda f: f.reshape(blocks, edge, rank)
+    shards = jax.ShapeDtypeStruct((blocks, edge, rank), BF16)
+    codes, rounds, shard_b, shard_c = pl.pallas_call(
         lambda *refs: plan(*refs, slots=slots, rows_count=rows_count, blocks=blocks),
         name="plan",
         out_shape=(
             jax.ShapeDtypeStruct((1, LANES), jnp.int32),
             jax.ShapeDtypeStruct((1, 1), jnp.int32),
+            shards,
+            shards,
         ),
-        in_specs=[pl.BlockSpec(memory_space=pltpu.HBM)] * 2,
-        out_specs=(vmem(), smem()),
+        in_specs=[pl.BlockSpec(memory_space=pltpu.HBM)] * 4,
+        out_specs=(vmem(), smem(), vmem(), vmem()),
         scratch_shapes=[
             pltpu.VMEM((1, tile_owner.shape[0]), jnp.int32),
             pltpu.VMEM((3, tile_owner.shape[0]), jnp.int32),
-            pltpu.SemaphoreType.DMA((2,)),
+            pltpu.SemaphoreType.DMA((4,)),
         ],
         compiler_params=LIMIT,
-    )(in_hbm(tile_owner.reshape(1, -1)), in_hbm(tile_coords.T))
-    by_block = lambda f: f.reshape(blocks, edge, rank)
+    )(
+        in_hbm(tile_owner.reshape(1, -1)),
+        in_hbm(tile_coords.T),
+        in_hbm(by_block(factor_b)),
+        in_hbm(by_block(factor_c)),
+    )
     sent = pl.pallas_call(
         lambda *refs: gather_factors(*refs, slots=slots),
         name="gather_factors",
         out_shape=tuple(jax.ShapeDtypeStruct((chips, c, edge, rank), BF16) for c in CAPACITIES),
         in_specs=[smem()] + [hbm()] * 4,
-        out_specs=(vmem(),) * len(CAPACITIES),
+        out_specs=(pl.BlockSpec(memory_space=pltpu.HBM),) * len(CAPACITIES),
         scratch_shapes=[pltpu.SemaphoreType.DMA],
         compiler_params=LIMIT,
     )(
         codes,
-        in_hbm(by_block(factor_b)),
-        in_hbm(by_block(factor_c)),
+        shard_b,
+        shard_c,
         by_block(sibling_b),
         by_block(sibling_c),
     )
     rest = lax.cond(rounds[0, 0] > 0, swap, lambda x: x, sent[1])
     first, rest = lax.optimization_barrier((sent[0], rest))
     chosen = [swap(first), rest]
-    own_b, own_c, sibling_b, sibling_c, *sent = lax.optimization_barrier(
-        (factor_b, factor_c, sibling_b, sibling_c, *sent)
+    own_x, own_b, own_c, sibling_b, sibling_c, *sent = lax.optimization_barrier(
+        (tile_values, factor_b, factor_c, sibling_b, sibling_c, *sent)
     )
     gram = pl.pallas_call(
         chip_gram,
@@ -417,13 +458,23 @@
         cost_estimate=SMALL,
     )(in_hbm(own_b), in_hbm(own_c), sibling_b, sibling_c)
     gram = gram + from_peer(gram, lambda q: q ^ CORES)
+    part = pl.pallas_call(
+        load_part,
+        name="load_part",
+        out_shape=jax.ShapeDtypeStruct((edge // 2, edge, edge), BF16),
+        in_specs=[pl.BlockSpec(memory_space=pltpu.HBM)],
+        out_specs=vmem(),
+        scratch_shapes=[pltpu.SemaphoreType.DMA],
+        compiler_params=LIMIT,
+        cost_estimate=SMALL,
+    )(in_hbm(own_x))
     chosen, gram = lax.optimization_barrier((chosen, gram))
 
     partials = pl.pallas_call(
         lambda *refs: contract(*refs, slots=slots, blocks=blocks),
         name="contract",
         out_shape=jax.ShapeDtypeStruct((tiles_count, slots) + tile, F32),
-        in_specs=[vmem(), pl.BlockSpec(memory_space=pltpu.HBM)] + [vmem()] * len(CAPACITIES),
+        in_specs=[vmem(), pl.BlockSpec(memory_space=pltpu.HBM), vmem()] + [vmem()] * len(CAPACITIES),
         out_specs=vmem(),
         scratch_shapes=[
             pltpu.VMEM(tile_values.shape, BF16),
@@ -435,21 +486,24 @@
         ],
         compiler_params=pltpu.CompilerParams(vmem_limit_bytes=24 << 20),
         cost_estimate=pl.CostEstimate(flops=slots * 2 * edge**4, bytes_accessed=slots * 2 * edge**3, transcendentals=0),
-    )(codes, in_hbm(tile_values), *chosen)
+    )(codes, in_hbm(tile_values), part, *chosen)
     moved = lax.all_to_all(partials, "tiles", 0, 0, tiled=True)
     gram = gram + from_peer(gram, lambda q: (chips - 1 - q // CORES) * CORES + q % CORES)
     moved, gram = lax.optimization_barrier((moved, gram))
-    dense = pl.pallas_call(
+    sums = jax.ShapeDtypeStruct((chips, blocks) + tile, F32)
+    keep, send = pl.pallas_call(
         lambda *refs: gather_blocks(*refs, slots=slots),
         name="gather_blocks",
-        out_shape=jax.ShapeDtypeStruct((rows_count, blocks) + tile, F32),
+        out_shape=(sums, sums),
         in_specs=[smem(), vmem()],
-        out_specs=vmem(),
+        out_specs=(vmem(), vmem()),
+        scratch_shapes=[pltpu.VMEM((CORES, chips, blocks) + tile, F32)],
         compiler_params=LIMIT,
     )(codes, moved)
-    dense, gram = lax.optimization_barrier((dense, gram))
+    send, gram = lax.optimization_barrier((send, gram))
     other = from_peer(gram, lambda q: q ^ 1)
-    owned = lax.all_to_all(dense, "rows", 0, 0, tiled=True)
+    summed, other = lax.optimization_barrier((keep + from_peer(send, lambda q: q ^ 1), other))
+    owned = swap(summed)
     inverse = pl.pallas_call(
         invert,
         name="invert",
@@ -473,7 +527,11 @@
         name="unpack",
         out_shape=jax.ShapeDtypeStruct((blocks, tiles_count) + tile, F32),
         in_specs=[vmem()],
-        out_specs=vmem(),
+        out_specs=pl.BlockSpec(memory_space=pltpu.HBM),
+        scratch_shapes=[
+            pltpu.VMEM((blocks, tiles_count) + tile, F32),
+            pltpu.SemaphoreType.DMA((4,)),
+        ],
         compiler_params=LIMIT,
     )(full)
     return out.reshape(shard, rank)

time: 82.5 us -> 78.4 us (0.950)
  waiting for transfers between devices: 20 us -> 15.6 us
  starting transfers between devices: 22.1 us -> 20.5 us
  Pallas kernels: 23.1 us -> 24 us
    all_to_all x1 -> x2, starting transfers between devices: 4.16 us -> 8.33 us  [swap(): return lax.all_to_all(x, 'rows', 0, 0, axis_index_groups=groups, tiled=True)]
    all_to_all x1, starting transfers between devices: 9.93 us -> 6.19 us  [body(): moved = lax.all_to_all(partials, 'tiles', 0, 0, tiled=True)]
    all_to_all x1 -> x0, starting transfers between devices: 3.49 us -> none  [body(): owned = lax.all_to_all(dense, 'rows', 0, 0, tiled=True)]
    all_to_all x1 -> x0, waiting for transfers between devices: 2.75 us -> none  [body(): owned = lax.all_to_all(dense, 'rows', 0, 0, tiled=True)]
    ppermute x5 -> x6, waiting for transfers between devices: 13.5 us -> 10.9 us  [from_peer(): return lax.ppermute(x, 'rows', [(q, peer(q)) for q in range(rows_count)])]
    pallas_call x0 -> x1, Pallas kernels: none -> 1.6 us  [body(): pl.pallas_call(load_part, name='load_part', out_shape=jax.ShapeDtypeStruc...]
    pallas_call x1, Pallas kernels: 2.83 us -> 1.36 us  [body(): pl.pallas_call(lambda *refs: gather_factors(*refs, slots=slots), name='ga...]
    ppermute x5 -> x6, starting transfers between devices: 4.5 us -> 5.93 us  [from_peer(): return lax.ppermute(x, 'rows', [(q, peer(q)) for q in range(rows_count)])]
  transfers between devices with their start and end apart: 8 -> 9, of which waited for: 6 -> 6; matrix products, arithmetic and copies ran while one was open for 0% -> 1% of each run, Pallas kernels for 12% -> 15%
where the time goes in v4:
time: 78.4 us; the launch traced here: 77 us
  Pallas kernels  24 us (31%)
  starting transfers between devices  20.5 us (26%)
  waiting for transfers between devices  15.6 us (20%)
  blocking collectives  15.3 us (20%)
    all_to_all x1, blocking collectives, body(): full = lax.all_to_all(solved, 'tiles', 0, 0, tiled=True)  15.3 us
    ppermute x6, waiting for transfers between devices, from_peer(): return lax.ppermute(x, 'rows', [(q, peer(q)) for q in range(rows_count)])  10.9 us
    all_to_all x2, starting transfers between devices, swap(): return lax.all_to_all(x, 'rows', 0, 0, axis_index_groups=groups, tiled=True)  8.33 us
    pallas_call x1, Pallas kernels, body(): pl.pallas_call(lambda *refs: contract(*refs, slots=slots, blocks=blocks),...  8.01 us
    all_to_all x1, starting transfers between devices, body(): moved = lax.all_to_all(partials, 'tiles', 0, 0, tiled=True)  6.19 us
    pallas_call x1, Pallas kernels, body(): pl.pallas_call(invert, name='invert', out_shape=jax.ShapeDtypeStruct((ran...  6.18 us
    ppermute x6, starting transfers between devices, from_peer(): return lax.ppermute(x, 'rows', [(q, peer(q)) for q in range(rows_count)])  5.93 us
    all_to_all x1, waiting for transfers between devices, body(): moved = lax.all_to_all(partials, 'tiles', 0, 0, tiled=True)  3.13 us
  transfers between devices with their start and end apart: 9, of which 6 were waited for; matrix products, arithmetic and copies ran while one was open for 1% of the time, Pallas kernels for 15%

profile of v4, /device:TPU:0, one launch (start us, length us, event | category | flops | bytes accessed | tf_op | source)
XLA Modules:
  0.0 77.0 jit_solution(114436132402379129)
XLA Ops:
  0.0 0.0 collective-permute-start
  0.0 0.5 collective-permute-start.1
  0.5 2.1 %plan.1 = (s32[1,128]{1,0:T(1,128)S(1)}, s32[1,1]{1,0:T(1,128)}, bf16[16,128,128]{2,1,0:T(8,128)(2,1)S(1)}, bf16[16,128,128]{2,1,0:T(8,128)(2,1)S(1)}) custom-call(s32[1,256]{1,0:T(1,128)} %bitcast.13, s32[3,256]{1,0:T(4,128)} %bitcast.12, bf16[16,128,128]{2,1,0:T(8,128)(2,1)} %bitcast.10, bf16[16,128,128]{2,1,0:T(8,128)(2,1)} %bitcast.11), custom_call_target="tpu_custom_call" | custom-call | tf_op jit(solution)/shard_map/plan/pallas_call | solution.py:403
  3.3 0.0 collective-permute-done.sb_ref
  3.3 0.0 collective-permute-done.1.sc_ref
  3.3 1.4 %gather_factors.1 = (bf16[4,6,128,128]{3,2,1,0:T(8,128)(2,1)}, bf16[4,2,128,128]{3,2,1,0:T(8,128)(2,1)S(1)}) custom-call(s32[1,128]{1,0:T(1,128)S(1)} %get-tuple-element.34.refs_0_, bf16[16,128,128]{2,1,0:T(8,128)(2,1)S(1)} %get-tuple-element.35.refs_1_, bf16[16,128,128]{2,1,0:T(8,128)(2,1)S(1)} %get-tuple-element.36.refs_2_, ...), custom_call_target="tpu_custom_call" | custom-call | tf_op jit(solution)/shard_map/gather_factors/pallas_call | solution.py:426
  4.7 4.6 %all-to-all-start.1 = ((bf16[4,6,128,128]{3,2,1,0:T(8,128)(2,1)}), bf16[4,6,128,128]{3,2,1,0:T(8,128)(2,1)S(1)}, u32[]{:S(2)}, u32[]{:S(2)}) async-start(bf16[4,6,128,128]{3,2,1,0:T(8,128)(2,1)} %get-tuple-element.41), calls=%async_computation.1 | async-start | bytes 1572864 | tf_op jit(solution)/shard_map/all_to_all | solution.py:398
  9.4 1.5 %chip_gram.1 = f32[128,128]{1,0:T(8,128)S(1)} custom-call(bf16[2048,128]{1,0:T(8,128)(2,1)} %fb_ref, bf16[2048,128]{1,0:T(8,128)(2,1)} %fc_ref, bf16[2048,128]{1,0:T(8,128)(2,1)S(1)} %collective-permute-done.sb_ref, bf16[2048,128]{1,0:T(8,128)(2,1)S(1)} %collective-permute-done.1.sc_ref), custom_call_target="tpu_custom_call" | custom-call | flops 1024 | bytes 1024 | tf_op jit(solution)/shard_map/chip_gram/pallas_call | solution.py:447
  10.9 2.1 %collective-permute-start.2 = (f32[128,128]{1,0:T(8,128)S(1)}, f32[128,128]{1,0:T(8,128)S(1)}, u32[]{:S(2)}, u32[]{:S(2)}) collective-permute-start(f32[128,128]{1,0:T(8,128)S(1)} %chip_gram.1), channel_id=1, source_target_pairs={{0,2},{1,3},{2,0},{3,1},{4,6},{5,7},{6,4},{7,5},{8,10},{9,11},{10,... | collective-permute-start | bytes 196616 | tf_op jit(solution)/shard_map/ppermute | solution.py:394
  13.0 1.6 %load_part.1.refs_2_ = bf16[64,128,128]{2,1,0:T(8,128)(2,1)S(1)} custom-call(bf16[4,128,128,128]{3,2,1,0:T(8,128)(2,1)} %refs_1_.1), custom_call_target="tpu_custom_call" | custom-call | flops 1024 | bytes 1024 | tf_op jit(solution)/shard_map/load_part/pallas_call | solution.py:461
  14.6 7.1 %collective-permute-done.2 = f32[128,128]{1,0:T(8,128)S(1)} collective-permute-done((f32[128,128]{1,0:T(8,128)S(1)}, f32[128,128]{1,0:T(8,128)S(1)}, u32[]{:S(2)}, u32[]{:S(2)}) %collective-permute-start.2) | collective-permute-done | bytes 65568 | tf_op jit(solution)/shard_map/ppermute | solution.py:394
  21.7 0.8 %all-to-all-done.1.refs_3_ = bf16[4,6,128,128]{3,2,1,0:T(8,128)(2,1)S(1)} async-done(((bf16[4,6,128,128]{3,2,1,0:T(8,128)(2,1)}), bf16[4,6,128,128]{3,2,1,0:T(8,128)(2,1)S(1)}, u32[]{:S(2)}, u32[]{:S(2)}) %all-to-all-start.1) | async-done | bytes 786464 | tf_op jit(solution)/shard_map/all_to_all | solution.py:398
  22.5 8.0 %contract.1 = f32[16,4,8,128]{3,2,1,0:T(8,128)} custom-call(s32[1,128]{1,0:T(1,128)S(1)} %get-tuple-element.34.refs_0_, bf16[4,128,128,128]{3,2,1,0:T(8,128)(2,1)} %refs_1_.1, bf16[64,128,128]{2,1,0:T(8,128)(2,1)S(1)} %load_part.1.refs_2_, bf16[4,6,128,128]{3,2,1,0:T(8,128)(2,1)S(1)} %all-to-all-done.1.refs_3_, ...), custom_call_target="tpu_custom_call" | custom-call | flops 2147483648 | bytes 16777216 | tf_op jit(solution)/shard_map/contract/pallas_call | solution.py:473
  30.5 6.2 %all-to-all-start.2 = ((f32[16,4,8,128]{3,2,1,0:T(8,128)}), f32[16,4,8,128]{3,2,1,0:T(8,128)S(1)}, u32[]{:S(2)}, u32[]{:S(2)}) async-start(f32[16,4,8,128]{3,2,1,0:T(8,128)} %contract.1), calls=%async_computation.2 | async-start | bytes 524288 | tf_op jit(solution)/shard_map/all_to_all | solution.py:490
  36.7 2.7 %collective-permute-start.3 = (f32[128,128]{1,0:T(8,128)S(1)}, f32[128,128]{1,0:T(8,128)S(1)}, u32[]{:S(2)}, u32[]{:S(2)}) collective-permute-start(f32[128,128]{1,0:T(8,128)S(1)} %add.9), channel_id=1, source_target_pairs={{0,6},{1,7},{2,4},{3,5},{4,2},{5,3},{6,0},{7,1},{8,14},{9,15},{10,... | collective-permute-start | bytes 196616 | tf_op jit(solution)/shard_map/ppermute | solution.py:394
  39.5 2.8 %collective-permute-done.3 = f32[128,128]{1,0:T(8,128)S(1)} collective-permute-done((f32[128,128]{1,0:T(8,128)S(1)}, f32[128,128]{1,0:T(8,128)S(1)}, u32[]{:S(2)}, u32[]{:S(2)}) %collective-permute-start.3) | collective-permute-done | bytes 65568 | tf_op jit(solution)/shard_map/ppermute | solution.py:394
  42.3 3.1 %all-to-all-done.2.refs_1_ = f32[16,4,8,128]{3,2,1,0:T(8,128)S(1)} async-done(((f32[16,4,8,128]{3,2,1,0:T(8,128)}), f32[16,4,8,128]{3,2,1,0:T(8,128)S(1)}, u32[]{:S(2)}, u32[]{:S(2)}) %all-to-all-start.2) | async-done | bytes 262176 | tf_op jit(solution)/shard_map/all_to_all | solution.py:490
  45.4 1.4 %gather_blocks.1 = (f32[4,16,8,128]{3,2,1,0:T(8,128)S(1)}, f32[4,16,8,128]{3,2,1,0:T(8,128)S(1)}) custom-call(s32[1,128]{1,0:T(1,128)S(1)} %get-tuple-element.34.refs_0_, f32[16,4,8,128]{3,2,1,0:T(8,128)S(1)} %all-to-all-done.2.refs_1_), custom_call_target="tpu_custom_call" | custom-call | tf_op jit(solution)/shard_map/gather_blocks/pallas_call | solution.py:494
  46.9 0.1 collective-permute-start.4
  46.9 0.5 collective-permute-start.5
  47.4 1.0 %collective-permute-done.4 = f32[4,16,8,128]{3,2,1,0:T(8,128)S(1)} collective-permute-done((f32[4,16,8,128]{3,2,1,0:T(8,128)S(1)}, f32[4,16,8,128]{3,2,1,0:T(8,128)S(1)}, u32[]{:S(2)}, u32[]{:S(2)}) %collective-permute-start.4) | collective-permute-done | bytes 262176 | tf_op jit(solution)/shard_map/ppermute | solution.py:394
  48.5 0.7 add.11
  49.2 0.0 collective-permute-done.5.other_ref
  49.2 3.7 %all-to-all-start.3 = ((f32[4,16,8,128]{3,2,1,0:T(8,128)}), f32[4,16,8,128]{3,2,1,0:T(8,128)S(1)}, u32[]{:S(2)}, u32[]{:S(2)}) async-start(f32[4,16,8,128]{3,2,1,0:T(8,128)} %add.11), calls=%async_computation.3 | async-start | bytes 524288 | tf_op jit(solution)/shard_map/all_to_all | solution.py:398
  52.9 6.2 %invert.1.inv_ref = f32[128,128]{1,0:T(8,128)S(1)} custom-call(f32[128,128]{1,0:T(8,128)S(1)} %add.10.one_ref, f32[128,128]{1,0:T(8,128)S(1)} %collective-permute-done.5.other_ref), custom_call_target="tpu_custom_call" | custom-call | flops 1073741824 | bytes 1048576 | tf_op jit(solution)/shard_map/invert/pallas_call | solution.py:507
  59.1 0.8 %all-to-all-done.3.in_ref = f32[4,16,8,128]{3,2,1,0:T(8,128)S(1)} async-done(((f32[4,16,8,128]{3,2,1,0:T(8,128)}), f32[4,16,8,128]{3,2,1,0:T(8,128)S(1)}, u32[]{:S(2)}, u32[]{:S(2)}) %all-to-all-start.3) | async-done | bytes 262176 | tf_op jit(solution)/shard_map/all_to_all | solution.py:398
  59.9 0.7 solve.1
  60.5 15.3 %all_to_all.25.in_ref = s16[16,17,8,128]{3,2,1,0:T(8,128)(2,1)S(1)} all-to-all(s16[16,17,8,128]{3,2,1,0:T(8,128)(2,1)S(1)} %solve.1), channel_id=1, replica_groups=mesh['tiles'=16,'rows'=8] {'tiles'}, dimensions={0} | all-to-all | bytes 1114112 | tf_op jit(solution)/shard_map/all_to_all | solution.py:524
  75.8 1.1 %unpack.1 = f32[16,16,8,128]{3,2,1,0:T(8,128)} custom-call(s16[16,17,8,128]{3,2,1,0:T(8,128)(2,1)S(1)} %all_to_all.25.in_ref), custom_call_target="tpu_custom_call" | custom-call | tf_op jit(solution)/shard_map/unpack/pallas_call | solution.py:525
  (4 shorter events, 0.1 us)
Async XLA Ops:
  0.0 3.3 %collective-permute-start = (bf16[2048,128]{1,0:T(8,128)(2,1)}, bf16[2048,128]{1,0:T(8,128)(2,1)S(1)}, u32[]{:S(2)}, u32[]{:S(2)}) collective-permute-start(bf16[2048,128]{1,0:T(8,128)(2,1)} %fb_ref), channel_id=1, source_target_pairs={{0,1},{1,0},{2,3},{3,2},{4,5},{5,4},{6,7},{7,6},{8,9},{9,8},{10,11... | collective-permute-start | bytes 1572872 | tf_op jit(solution)/shard_map/ppermute | solution.py:394
  0.0 3.3 %collective-permute-start.1 = (bf16[2048,128]{1,0:T(8,128)(2,1)}, bf16[2048,128]{1,0:T(8,128)(2,1)S(1)}, u32[]{:S(2)}, u32[]{:S(2)}) collective-permute-start(bf16[2048,128]{1,0:T(8,128)(2,1)} %fc_ref), channel_id=1, source_target_pairs={{0,1},{1,0},{2,3},{3,2},{4,5},{5,4},{6,7},{7,6},{8,9},{9,8},{10,11... | collective-permute-start | bytes 1572872 | tf_op jit(solution)/shard_map/ppermute | solution.py:394
  4.7 17.8 %all-to-all-start.1 = ((bf16[4,6,128,128]{3,2,1,0:T(8,128)(2,1)}), bf16[4,6,128,128]{3,2,1,0:T(8,128)(2,1)S(1)}, u32[]{:S(2)}, u32[]{:S(2)}) async-start(bf16[4,6,128,128]{3,2,1,0:T(8,128)(2,1)} %get-tuple-element.41), calls=%async_computation.1 | async-start | bytes 1572864 | tf_op jit(solution)/shard_map/all_to_all | solution.py:398
  10.9 10.8 %collective-permute-start.2 = (f32[128,128]{1,0:T(8,128)S(1)}, f32[128,128]{1,0:T(8,128)S(1)}, u32[]{:S(2)}, u32[]{:S(2)}) collective-permute-start(f32[128,128]{1,0:T(8,128)S(1)} %chip_gram.1), channel_id=1, source_target_pairs={{0,2},{1,3},{2,0},{3,1},{4,6},{5,7},{6,4},{7,5},{8,10},{9,11},{10,... | collective-permute-start | bytes 196616 | tf_op jit(solution)/shard_map/ppermute | solution.py:394
  30.5 14.9 %all-to-all-start.2 = ((f32[16,4,8,128]{3,2,1,0:T(8,128)}), f32[16,4,8,128]{3,2,1,0:T(8,128)S(1)}, u32[]{:S(2)}, u32[]{:S(2)}) async-start(f32[16,4,8,128]{3,2,1,0:T(8,128)} %contract.1), calls=%async_computation.2 | async-start | bytes 524288 | tf_op jit(solution)/shard_map/all_to_all | solution.py:490
  36.7 5.6 %collective-permute-start.3 = (f32[128,128]{1,0:T(8,128)S(1)}, f32[128,128]{1,0:T(8,128)S(1)}, u32[]{:S(2)}, u32[]{:S(2)}) collective-permute-start(f32[128,128]{1,0:T(8,128)S(1)} %add.9), channel_id=1, source_target_pairs={{0,6},{1,7},{2,4},{3,5},{4,2},{5,3},{6,0},{7,1},{8,14},{9,15},{10,... | collective-permute-start | bytes 196616 | tf_op jit(solution)/shard_map/ppermute | solution.py:394
  46.9 1.6 %collective-permute-start.4 = (f32[4,16,8,128]{3,2,1,0:T(8,128)S(1)}, f32[4,16,8,128]{3,2,1,0:T(8,128)S(1)}, u32[]{:S(2)}, u32[]{:S(2)}) collective-permute-start(f32[4,16,8,128]{3,2,1,0:T(8,128)S(1)} %get-tuple-element.54), channel_id=1, source_target_pairs={{0,1},{1,0},{2,3},{3,2},{4,5},{5,4},{6,7},{7,6},{8,9},{9,8},{10,11... | collective-permute-start | bytes 786440 | tf_op jit(solution)/shard_map/ppermute | solution.py:394
  46.9 2.3 %collective-permute-start.5 = (f32[128,128]{1,0:T(8,128)S(1)}, f32[128,128]{1,0:T(8,128)S(1)}, u32[]{:S(2)}, u32[]{:S(2)}) collective-permute-start(f32[128,128]{1,0:T(8,128)S(1)} %add.10.one_ref), channel_id=1, source_target_pairs={{0,1},{1,0},{2,3},{3,2},{4,5},{5,4},{6,7},{7,6},{8,9},{9,8},{10,11... | collective-permute-start | bytes 196616 | tf_op jit(solution)/shard_map/ppermute | solution.py:394
  49.2 10.7 %all-to-all-start.3 = ((f32[4,16,8,128]{3,2,1,0:T(8,128)}), f32[4,16,8,128]{3,2,1,0:T(8,128)S(1)}, u32[]{:S(2)}, u32[]{:S(2)}) async-start(f32[4,16,8,128]{3,2,1,0:T(8,128)} %add.11), calls=%async_computation.3 | async-start | bytes 524288 | tf_op jit(solution)/shard_map/all_to_all | solution.py:398

commit v5 on v4

--- a/solution.py
+++ b/solution.py
@@ -181,7 +181,7 @@
 
 def contract(code_ref, x_ref, part_ref, *refs, slots, blocks):
     ins = refs[: len(CAPACITIES)]
-    out_ref, buf, bs, cs, scalar_ref, code_sem, sem = refs[len(CAPACITIES) :]
+    out_hbm, out_ref, buf, bs, cs, scalar_ref, code_sem, sem, out_sem = refs[len(CAPACITIES) :]
     r = lax.axis_index("rows")
     edge = x_ref.shape[1]
     part = edge // PARTS
@@ -223,7 +223,15 @@
                 value = held if value is None else jnp.where(inside, held, value)
                 base = base + capacity
             keep[s] = value.astype(keep.dtype)
+    def store(s):
+        return pltpu.make_async_copy(out_ref.at[:, s], out_hbm.at[:, s], out_sem.at[s])
+
     out_ref[...] = jnp.zeros_like(out_ref)
+    for s in range(slots):
+
+        @pl.when(s >= live)
+        def _(s=s):
+            store(s).start()
 
     def multiply(s, q):
         b = bs[s]
@@ -240,6 +248,7 @@
             fetch(s, q).wait()
         for q in range(PARTS):
             multiply(s, q)
+        store(s).start()
         return carry
 
     last = live - 1
@@ -250,6 +259,7 @@
         for q in range(PARTS):
             fetch(last, q).wait()
             multiply(last, q)
+        store(last).start()
 
     def drain(s, carry):
         for q in range(PARTS):
@@ -257,6 +267,8 @@
         return carry
 
     lax.fori_loop(live, slots, drain, 0)
+    for s in range(slots):
+        store(s).wait()
 
 
 def eliminate(matrix):
@@ -475,14 +487,16 @@
         name="contract",
         out_shape=jax.ShapeDtypeStruct((tiles_count, slots) + tile, F32),
         in_specs=[vmem(), pl.BlockSpec(memory_space=pltpu.HBM), vmem()] + [vmem()] * len(CAPACITIES),
-        out_specs=vmem(),
+        out_specs=pl.BlockSpec(memory_space=pltpu.HBM),
         scratch_shapes=[
+            pltpu.VMEM((tiles_count, slots) + tile, F32),
             pltpu.VMEM(tile_values.shape, BF16),
             pltpu.VMEM((slots, edge, rank), F32),
             pltpu.VMEM((slots, edge, rank), BF16),
             pltpu.SMEM((1, LANES), jnp.int32),
             pltpu.SemaphoreType.DMA,
             pltpu.SemaphoreType.DMA((slots, PARTS)),
+            pltpu.SemaphoreType.DMA((slots,)),
         ],
         compiler_params=pltpu.CompilerParams(vmem_limit_bytes=24 << 20),
         cost_estimate=pl.CostEstimate(flops=slots * 2 * edge**4, bytes_accessed=slots * 2 * edge**3, transcendentals=0),

time: 78.4 us -> 78.8 us (level); the launches traced: 77 us -> 78.3 us
  Pallas kernels: 24 us -> 21.8 us
  starting transfers between devices: 20.5 us -> 22.7 us
  waiting for transfers between devices: 15.6 us -> 16.9 us
    all_to_all x1, starting transfers between devices: 6.19 us -> 10.1 us  [body(): moved = lax.all_to_all(partials, 'tiles', 0, 0, tiled=True)]
    pallas_call x1, Pallas kernels: 8.01 us -> 5.59 us  [body(): pl.pallas_call(lambda *refs: contract(*refs, slots=slots, blocks=blocks),...]
    ppermute x6, waiting for transfers between devices: 10.9 us -> 12.3 us  [from_peer(): return lax.ppermute(x, 'rows', [(q, peer(q)) for q in range(rows_count)])]
    ppermute x6, starting transfers between devices: 5.93 us -> 4.64 us  [from_peer(): return lax.ppermute(x, 'rows', [(q, peer(q)) for q in range(rows_count)])]
where the time goes in v5:
time: 78.8 us; the launch traced here: 78.3 us
  starting transfers between devices  22.7 us (29%)
  Pallas kernels  21.8 us (28%)
  waiting for transfers between devices  16.9 us (21%)
  blocking collectives  15.3 us (19%)
    all_to_all x1, blocking collectives, body(): full = lax.all_to_all(solved, 'tiles', 0, 0, tiled=True)  15.3 us
    ppermute x6, waiting for transfers between devices, from_peer(): return lax.ppermute(x, 'rows', [(q, peer(q)) for q in range(rows_count)])  12.3 us
    all_to_all x1, starting transfers between devices, body(): moved = lax.all_to_all(partials, 'tiles', 0, 0, tiled=True)  10.1 us
    all_to_all x2, starting transfers between devices, swap(): return lax.all_to_all(x, 'rows', 0, 0, axis_index_groups=groups, tiled=True)  7.92 us
    pallas_call x1, Pallas kernels, body(): pl.pallas_call(invert, name='invert', out_shape=jax.ShapeDtypeStruct((ran...  6.18 us
    pallas_call x1, Pallas kernels, body(): pl.pallas_call(lambda *refs: contract(*refs, slots=slots, blocks=blocks),...  5.59 us
    ppermute x6, starting transfers between devices, from_peer(): return lax.ppermute(x, 'rows', [(q, peer(q)) for q in range(rows_count)])  4.64 us
    all_to_all x1, waiting for transfers between devices, body(): moved = lax.all_to_all(partials, 'tiles', 0, 0, tiled=True)  2.9 us
  transfers between devices with their start and end apart: 9, of which 6 were waited for; matrix products, arithmetic and copies ran while one was open for 1% of the time, Pallas kernels for 15%

profile of v5, /device:TPU:0, one launch (start us, length us, event | category | flops | bytes accessed | tf_op | source)
XLA Modules:
  0.0 78.3 jit_solution(3849183539385074432)
XLA Ops:
  0.0 0.0 collective-permute-start
  0.0 0.5 collective-permute-start.1
  0.5 2.1 %plan.1 = (s32[1,128]{1,0:T(1,128)S(1)}, s32[1,1]{1,0:T(1,128)}, bf16[16,128,128]{2,1,0:T(8,128)(2,1)S(1)}, bf16[16,128,128]{2,1,0:T(8,128)(2,1)S(1)}) custom-call(s32[1,256]{1,0:T(1,128)} %bitcast.13, s32[3,256]{1,0:T(4,128)} %bitcast.12, bf16[16,128,128]{2,1,0:T(8,128)(2,1)} %bitcast.10, bf16[16,128,128]{2,1,0:T(8,128)(2,1)} %bitcast.11), custom_call_target="tpu_custom_call" | custom-call | tf_op jit(solution)/shard_map/plan/pallas_call | solution.py:415
  3.3 0.0 collective-permute-done.sb_ref
  3.3 0.0 collective-permute-done.1.sc_ref
  3.3 1.6 %gather_factors.1 = (bf16[4,6,128,128]{3,2,1,0:T(8,128)(2,1)}, bf16[4,2,128,128]{3,2,1,0:T(8,128)(2,1)S(1)}) custom-call(s32[1,128]{1,0:T(1,128)S(1)} %get-tuple-element.34.refs_0_, bf16[16,128,128]{2,1,0:T(8,128)(2,1)S(1)} %get-tuple-element.35.refs_1_, bf16[16,128,128]{2,1,0:T(8,128)(2,1)S(1)} %get-tuple-element.36.refs_2_, ...), custom_call_target="tpu_custom_call" | custom-call | tf_op jit(solution)/shard_map/gather_factors/pallas_call | solution.py:438
  4.9 4.4 %all-to-all-start.1 = ((bf16[4,6,128,128]{3,2,1,0:T(8,128)(2,1)}), bf16[4,6,128,128]{3,2,1,0:T(8,128)(2,1)S(1)}, u32[]{:S(2)}, u32[]{:S(2)}) async-start(bf16[4,6,128,128]{3,2,1,0:T(8,128)(2,1)} %get-tuple-element.41), calls=%async_computation.1 | async-start | bytes 1572864 | tf_op jit(solution)/shard_map/all_to_all | solution.py:410
  9.3 1.5 %chip_gram.1 = f32[128,128]{1,0:T(8,128)S(1)} custom-call(bf16[2048,128]{1,0:T(8,128)(2,1)} %fb_ref, bf16[2048,128]{1,0:T(8,128)(2,1)} %fc_ref, bf16[2048,128]{1,0:T(8,128)(2,1)S(1)} %collective-permute-done.sb_ref, bf16[2048,128]{1,0:T(8,128)(2,1)S(1)} %collective-permute-done.1.sc_ref), custom_call_target="tpu_custom_call" | custom-call | flops 1024 | bytes 1024 | tf_op jit(solution)/shard_map/chip_gram/pallas_call | solution.py:459
  10.9 2.1 %collective-permute-start.2 = (f32[128,128]{1,0:T(8,128)S(1)}, f32[128,128]{1,0:T(8,128)S(1)}, u32[]{:S(2)}, u32[]{:S(2)}) collective-permute-start(f32[128,128]{1,0:T(8,128)S(1)} %chip_gram.1), channel_id=1, source_target_pairs={{0,2},{1,3},{2,0},{3,1},{4,6},{5,7},{6,4},{7,5},{8,10},{9,11},{10,... | collective-permute-start | bytes 196616 | tf_op jit(solution)/shard_map/ppermute | solution.py:406
  13.0 1.6 %load_part.1.refs_2_ = bf16[64,128,128]{2,1,0:T(8,128)(2,1)S(1)} custom-call(bf16[4,128,128,128]{3,2,1,0:T(8,128)(2,1)} %refs_1_.1), custom_call_target="tpu_custom_call" | custom-call | flops 1024 | bytes 1024 | tf_op jit(solution)/shard_map/load_part/pallas_call | solution.py:473
  14.6 7.1 %collective-permute-done.2 = f32[128,128]{1,0:T(8,128)S(1)} collective-permute-done((f32[128,128]{1,0:T(8,128)S(1)}, f32[128,128]{1,0:T(8,128)S(1)}, u32[]{:S(2)}, u32[]{:S(2)}) %collective-permute-start.2) | collective-permute-done | bytes 65568 | tf_op jit(solution)/shard_map/ppermute | solution.py:406
  21.7 0.8 %all-to-all-done.1.refs_3_ = bf16[4,6,128,128]{3,2,1,0:T(8,128)(2,1)S(1)} async-done(((bf16[4,6,128,128]{3,2,1,0:T(8,128)(2,1)}), bf16[4,6,128,128]{3,2,1,0:T(8,128)(2,1)S(1)}, u32[]{:S(2)}, u32[]{:S(2)}) %all-to-all-start.1) | async-done | bytes 786464 | tf_op jit(solution)/shard_map/all_to_all | solution.py:410
  22.5 5.6 %contract.1 = f32[16,4,8,128]{3,2,1,0:T(8,128)} custom-call(s32[1,128]{1,0:T(1,128)S(1)} %get-tuple-element.34.refs_0_, bf16[4,128,128,128]{3,2,1,0:T(8,128)(2,1)} %refs_1_.1, bf16[64,128,128]{2,1,0:T(8,128)(2,1)S(1)} %load_part.1.refs_2_, bf16[4,6,128,128]{3,2,1,0:T(8,128)(2,1)S(1)} %all-to-all-done.1.refs_3_, ...), custom_call_target="tpu_custom_call" | custom-call | flops 2147483648 | bytes 16777216 | tf_op jit(solution)/shard_map/contract/pallas_call | solution.py:485
  28.1 10.1 %all-to-all-start.2 = ((f32[16,4,8,128]{3,2,1,0:T(8,128)}), f32[16,4,8,128]{3,2,1,0:T(8,128)S(1)}, u32[]{:S(2)}, u32[]{:S(2)}) async-start(f32[16,4,8,128]{3,2,1,0:T(8,128)} %contract.1), calls=%async_computation.2 | async-start | bytes 524288 | tf_op jit(solution)/shard_map/all_to_all | solution.py:504
  38.2 1.4 %collective-permute-start.3 = (f32[128,128]{1,0:T(8,128)S(1)}, f32[128,128]{1,0:T(8,128)S(1)}, u32[]{:S(2)}, u32[]{:S(2)}) collective-permute-start(f32[128,128]{1,0:T(8,128)S(1)} %add.9), channel_id=1, source_target_pairs={{0,6},{1,7},{2,4},{3,5},{4,2},{5,3},{6,0},{7,1},{8,14},{9,15},{10,... | collective-permute-start | bytes 196616 | tf_op jit(solution)/shard_map/ppermute | solution.py:406
  39.7 4.1 %collective-permute-done.3 = f32[128,128]{1,0:T(8,128)S(1)} collective-permute-done((f32[128,128]{1,0:T(8,128)S(1)}, f32[128,128]{1,0:T(8,128)S(1)}, u32[]{:S(2)}, u32[]{:S(2)}) %collective-permute-start.3) | collective-permute-done | bytes 65568 | tf_op jit(solution)/shard_map/ppermute | solution.py:406
  43.8 2.9 %all-to-all-done.2.refs_1_ = f32[16,4,8,128]{3,2,1,0:T(8,128)S(1)} async-done(((f32[16,4,8,128]{3,2,1,0:T(8,128)}), f32[16,4,8,128]{3,2,1,0:T(8,128)S(1)}, u32[]{:S(2)}, u32[]{:S(2)}) %all-to-all-start.2) | async-done | bytes 262176 | tf_op jit(solution)/shard_map/all_to_all | solution.py:504
  46.7 1.4 %gather_blocks.1 = (f32[4,16,8,128]{3,2,1,0:T(8,128)S(1)}, f32[4,16,8,128]{3,2,1,0:T(8,128)S(1)}) custom-call(s32[1,128]{1,0:T(1,128)S(1)} %get-tuple-element.34.refs_0_, f32[16,4,8,128]{3,2,1,0:T(8,128)S(1)} %all-to-all-done.2.refs_1_), custom_call_target="tpu_custom_call" | custom-call | tf_op jit(solution)/shard_map/gather_blocks/pallas_call | solution.py:508
  48.2 0.1 collective-permute-start.4
  48.2 0.5 collective-permute-start.5
  48.7 1.0 %collective-permute-done.4 = f32[4,16,8,128]{3,2,1,0:T(8,128)S(1)} collective-permute-done((f32[4,16,8,128]{3,2,1,0:T(8,128)S(1)}, f32[4,16,8,128]{3,2,1,0:T(8,128)S(1)}, u32[]{:S(2)}, u32[]{:S(2)}) %collective-permute-start.4) | collective-permute-done | bytes 262176 | tf_op jit(solution)/shard_map/ppermute | solution.py:406
  49.8 0.7 add.11
  50.5 0.0 collective-permute-done.5.other_ref
  50.5 3.5 %all-to-all-start.3 = ((f32[4,16,8,128]{3,2,1,0:T(8,128)}), f32[4,16,8,128]{3,2,1,0:T(8,128)S(1)}, u32[]{:S(2)}, u32[]{:S(2)}) async-start(f32[4,16,8,128]{3,2,1,0:T(8,128)} %add.11), calls=%async_computation.3 | async-start | bytes 524288 | tf_op jit(solution)/shard_map/all_to_all | solution.py:410
  54.0 6.2 %invert.1.inv_ref = f32[128,128]{1,0:T(8,128)S(1)} custom-call(f32[128,128]{1,0:T(8,128)S(1)} %add.10.one_ref, f32[128,128]{1,0:T(8,128)S(1)} %collective-permute-done.5.other_ref), custom_call_target="tpu_custom_call" | custom-call | flops 1073741824 | bytes 1048576 | tf_op jit(solution)/shard_map/invert/pallas_call | solution.py:521
  60.2 0.9 %all-to-all-done.3.in_ref = f32[4,16,8,128]{3,2,1,0:T(8,128)S(1)} async-done(((f32[4,16,8,128]{3,2,1,0:T(8,128)}), f32[4,16,8,128]{3,2,1,0:T(8,128)S(1)}, u32[]{:S(2)}, u32[]{:S(2)}) %all-to-all-start.3) | async-done | bytes 262176 | tf_op jit(solution)/shard_map/all_to_all | solution.py:410
  61.1 0.7 solve.1
  61.8 15.3 %all_to_all.25.in_ref = s16[16,17,8,128]{3,2,1,0:T(8,128)(2,1)S(1)} all-to-all(s16[16,17,8,128]{3,2,1,0:T(8,128)(2,1)S(1)} %solve.1), channel_id=1, replica_groups=mesh['tiles'=16,'rows'=8] {'tiles'}, dimensions={0} | all-to-all | bytes 1114112 | tf_op jit(solution)/shard_map/all_to_all | solution.py:538
  77.1 1.1 %unpack.1 = f32[16,16,8,128]{3,2,1,0:T(8,128)} custom-call(s16[16,17,8,128]{3,2,1,0:T(8,128)(2,1)S(1)} %all_to_all.25.in_ref), custom_call_target="tpu_custom_call" | custom-call | tf_op jit(solution)/shard_map/unpack/pallas_call | solution.py:539
  (4 shorter events, 0.1 us)
Async XLA Ops:
  0.0 3.3 %collective-permute-start = (bf16[2048,128]{1,0:T(8,128)(2,1)}, bf16[2048,128]{1,0:T(8,128)(2,1)S(1)}, u32[]{:S(2)}, u32[]{:S(2)}) collective-permute-start(bf16[2048,128]{1,0:T(8,128)(2,1)} %fb_ref), channel_id=1, source_target_pairs={{0,1},{1,0},{2,3},{3,2},{4,5},{5,4},{6,7},{7,6},{8,9},{9,8},{10,11... | collective-permute-start | bytes 1572872 | tf_op jit(solution)/shard_map/ppermute | solution.py:406
  0.0 3.3 %collective-permute-start.1 = (bf16[2048,128]{1,0:T(8,128)(2,1)}, bf16[2048,128]{1,0:T(8,128)(2,1)S(1)}, u32[]{:S(2)}, u32[]{:S(2)}) collective-permute-start(bf16[2048,128]{1,0:T(8,128)(2,1)} %fc_ref), channel_id=1, source_target_pairs={{0,1},{1,0},{2,3},{3,2},{4,5},{5,4},{6,7},{7,6},{8,9},{9,8},{10,11... | collective-permute-start | bytes 1572872 | tf_op jit(solution)/shard_map/ppermute | solution.py:406
  4.9 17.6 %all-to-all-start.1 = ((bf16[4,6,128,128]{3,2,1,0:T(8,128)(2,1)}), bf16[4,6,128,128]{3,2,1,0:T(8,128)(2,1)S(1)}, u32[]{:S(2)}, u32[]{:S(2)}) async-start(bf16[4,6,128,128]{3,2,1,0:T(8,128)(2,1)} %get-tuple-element.41), calls=%async_computation.1 | async-start | bytes 1572864 | tf_op jit(solution)/shard_map/all_to_all | solution.py:410
  10.9 10.8 %collective-permute-start.2 = (f32[128,128]{1,0:T(8,128)S(1)}, f32[128,128]{1,0:T(8,128)S(1)}, u32[]{:S(2)}, u32[]{:S(2)}) collective-permute-start(f32[128,128]{1,0:T(8,128)S(1)} %chip_gram.1), channel_id=1, source_target_pairs={{0,2},{1,3},{2,0},{3,1},{4,6},{5,7},{6,4},{7,5},{8,10},{9,11},{10,... | collective-permute-start | bytes 196616 | tf_op jit(solution)/shard_map/ppermute | solution.py:406
  28.1 18.6 %all-to-all-start.2 = ((f32[16,4,8,128]{3,2,1,0:T(8,128)}), f32[16,4,8,128]{3,2,1,0:T(8,128)S(1)}, u32[]{:S(2)}, u32[]{:S(2)}) async-start(f32[16,4,8,128]{3,2,1,0:T(8,128)} %contract.1), calls=%async_computation.2 | async-start | bytes 524288 | tf_op jit(solution)/shard_map/all_to_all | solution.py:504
  38.2 5.6 %collective-permute-start.3 = (f32[128,128]{1,0:T(8,128)S(1)}, f32[128,128]{1,0:T(8,128)S(1)}, u32[]{:S(2)}, u32[]{:S(2)}) collective-permute-start(f32[128,128]{1,0:T(8,128)S(1)} %add.9), channel_id=1, source_target_pairs={{0,6},{1,7},{2,4},{3,5},{4,2},{5,3},{6,0},{7,1},{8,14},{9,15},{10,... | collective-permute-start | bytes 196616 | tf_op jit(solution)/shard_map/ppermute | solution.py:406
  48.2 1.6 %collective-permute-start.4 = (f32[4,16,8,128]{3,2,1,0:T(8,128)S(1)}, f32[4,16,8,128]{3,2,1,0:T(8,128)S(1)}, u32[]{:S(2)}, u32[]{:S(2)}) collective-permute-start(f32[4,16,8,128]{3,2,1,0:T(8,128)S(1)} %get-tuple-element.54), channel_id=1, source_target_pairs={{0,1},{1,0},{2,3},{3,2},{4,5},{5,4},{6,7},{7,6},{8,9},{9,8},{10,11... | collective-permute-start | bytes 786440 | tf_op jit(solution)/shard_map/ppermute | solution.py:406
  48.2 2.3 %collective-permute-start.5 = (f32[128,128]{1,0:T(8,128)S(1)}, f32[128,128]{1,0:T(8,128)S(1)}, u32[]{:S(2)}, u32[]{:S(2)}) collective-permute-start(f32[128,128]{1,0:T(8,128)S(1)} %add.10.one_ref), channel_id=1, source_target_pairs={{0,1},{1,0},{2,3},{3,2},{4,5},{5,4},{6,7},{7,6},{8,9},{9,8},{10,11... | collective-permute-start | bytes 196616 | tf_op jit(solution)/shard_map/ppermute | solution.py:406
  50.5 10.6 %all-to-all-start.3 = ((f32[4,16,8,128]{3,2,1,0:T(8,128)}), f32[4,16,8,128]{3,2,1,0:T(8,128)S(1)}, u32[]{:S(2)}, u32[]{:S(2)}) async-start(f32[4,16,8,128]{3,2,1,0:T(8,128)} %add.11), calls=%async_computation.3 | async-start | bytes 524288 | tf_op jit(solution)/shard_map/all_to_all | solution.py:410
